TPU v7x, 32 devices: a whole 2x2x4 slice. The times are simulated.
32 devices in a mesh: dp: 4 (over y, x), ctx: 8 (over z, core).
Axes of the slice: x: 2, y: 2, z: 4, core: 2. Of those that a mesh axis runs over, the one named last changes fastest.
Arguments:
- stream: bfloat16 [16, 4096, 1600], P('dp', 'ctx'), may hold values from -16 to 16
- segments: int32 [16, 4096], P('dp'), may hold values from 0 to 3, never falling along the last dimension, each value on 1 to 2000 neighbouring positions
- cotangent: bfloat16 [16, 4096, 1600], P('dp', 'ctx'), may hold values from -6 to 6
- gain_zero: bfloat16 [1600], P('dp'), may hold values from 0.099609375 to 1.8984375
- shift_zero: bfloat16 [1600], P('dp'), may hold values from -2.390625 to 2.390625
- weight_in: bfloat16 [1600, 800], P('dp'), may hold values from -0.21875 to 0.21875
- bias_in: bfloat16 [800], P('dp'), may hold values from -3 to 3
- gain_one: bfloat16 [800], P('dp'), may hold values from 0.099609375 to 1.8984375
- shift_one: bfloat16 [800], P('dp'), may hold values from -2.390625 to 2.390625
- weight_conv: bfloat16 [3, 800, 800], P(None, 'dp'), may hold values from -0.15625 to 0.15625
- bias_conv: bfloat16 [800], P('dp'), may hold values from -3 to 3
- gain_two: bfloat16 [800], P('dp'), may hold values from 0.099609375 to 1.8984375
- shift_two: bfloat16 [800], P('dp'), may hold values from -2.390625 to 2.390625
- weight_out: bfloat16 [800, 1600], P('dp'), may hold values from -0.3125 to 0.3125
- bias_out: bfloat16 [1600], P('dp'), may hold values from -3 to 3
Outputs:
- output: bfloat16 [16, 4096, 1600], P('dp', 'ctx')
- grad_stream: bfloat16 [16, 4096, 1600], P('dp', 'ctx')
- grad_gain_zero: float32 [1600], P('dp')
- grad_shift_zero: float32 [1600], P('dp')
- grad_weight_in: float32 [1600, 800], P('dp')
- grad_bias_in: float32 [800], P('dp')
- grad_gain_one: float32 [800], P('dp')
- grad_shift_one: float32 [800], P('dp')
- grad_weight_conv: float32 [3, 800, 800], P(None, 'dp')
- grad_bias_conv: float32 [800], P('dp')
- grad_gain_two: float32 [800], P('dp')
- grad_shift_two: float32 [800], P('dp')
- grad_weight_out: float32 [800, 1600], P('dp')
- grad_bias_out: float32 [1600], P('dp')
- rms_in: float32 [], replicated
- rms_out: float32 [], replicated
- rms_hidden_one: float32 [], replicated
- rms_hidden_two: float32 [], replicated
- rms_branch: float32 [], replicated
All inputs are finite; a program needn't handle non-finite values.
Results may differ from a plain program's by a relative error of at most 0.0066.
Values may be sent and summed in bfloat16 or wider, within the bound.
No kernel may reach another device: no remote copies, remote signals or barrier semaphores. Data moves between devices by JAX's collectives and lax.ppermute only.
A program may use at most 256 MiB of HBM per device.

v0:
```python
import jax
import jax.numpy as jnp
from jax import lax
from jax.sharding import PartitionSpec as P


def shifted(value, axis, by):
    size = lax.axis_size(axis)
    pairs = [(i, i + by) for i in range(size) if 0 <= i + by < size]
    return lax.ppermute(value, axis, pairs)


def smooth_act(values):
    return values * jax.nn.sigmoid(values)


def layer_stats(values, gain_vec, shift_vec):
    average = jnp.mean(values, axis=-1, keepdims=True)
    centred = values - average
    inverse = lax.rsqrt(jnp.mean(centred * centred, axis=-1, keepdims=True) + 1e-05)
    normed = centred * inverse
    return (normed, inverse, normed * gain_vec + shift_vec)


def norm_back(grad_act, normed, inverse, pre_act, gain_vec):
    sigma = jax.nn.sigmoid(pre_act)
    grad_pre = grad_act * sigma * (1.0 + pre_act * (1.0 - sigma))
    grad_gain = jnp.sum(grad_pre * normed, axis=0)
    grad_shift = jnp.sum(grad_pre, axis=0)
    grad_norm = grad_pre * gain_vec
    grad_in = (
        grad_norm
        - jnp.mean(grad_norm, axis=-1, keepdims=True)
        - normed * jnp.mean(grad_norm * normed, axis=-1, keepdims=True)
    ) * inverse
    return (grad_in, grad_gain, grad_shift)


def local(
    stream,
    segments,
    cotangent,
    gain_zero,
    shift_zero,
    weight_in,
    bias_in,
    gain_one,
    shift_one,
    weight_conv,
    bias_conv,
    gain_two,
    shift_two,
    weight_out,
    bias_out,
):
    gathered = (
        lax.all_gather(gain_zero, "dp", axis=0, tiled=True),
        lax.all_gather(shift_zero, "dp", axis=0, tiled=True),
        lax.all_gather(weight_in, "dp", axis=0, tiled=True),
        lax.all_gather(bias_in, "dp", axis=0, tiled=True),
        lax.all_gather(gain_one, "dp", axis=0, tiled=True),
        lax.all_gather(shift_one, "dp", axis=0, tiled=True),
        lax.all_gather(weight_conv, "dp", axis=1, tiled=True),
        lax.all_gather(bias_conv, "dp", axis=0, tiled=True),
        lax.all_gather(gain_two, "dp", axis=0, tiled=True),
        lax.all_gather(shift_two, "dp", axis=0, tiled=True),
        lax.all_gather(weight_out, "dp", axis=0, tiled=True),
        lax.all_gather(bias_out, "dp", axis=0, tiled=True),
    )
    (
        full_g0,
        full_e0,
        full_win,
        full_bin,
        full_g1,
        full_e1,
        full_wconv,
        full_bconv,
        full_g2,
        full_e2,
        full_wout,
        full_bout,
    ) = gathered
    g0_f = full_g0.astype(jnp.float32)
    e0_f = full_e0.astype(jnp.float32)
    g1_f = full_g1.astype(jnp.float32)
    e1_f = full_e1.astype(jnp.float32)
    g2_f = full_g2.astype(jnp.float32)
    e2_f = full_e2.astype(jnp.float32)
    seq_local, block_rows, wide_dim = stream.shape
    inner = full_wconv.shape[1]
    row_count = seq_local * block_rows
    conv_flat = full_wconv.reshape(3 * inner, inner)
    first_row = lax.axis_index("ctx") * block_rows
    own_segs = lax.dynamic_slice_in_dim(segments, first_row, block_rows, 1)
    prior_segs = lax.dynamic_slice_in_dim(segments, jnp.maximum(first_row - 4, 0), 4, 1)
    seg_ext = jnp.concatenate([prior_segs, own_segs], axis=1)
    flat_rows = stream.reshape(row_count, wide_dim).astype(jnp.float32)
    normed0, inverse0, pre0 = layer_stats(flat_rows, g0_f, e0_f)
    act_zero = smooth_act(pre0).astype(jnp.bfloat16)
    hidden_one = jnp.dot(act_zero, full_win, preferred_element_type=jnp.float32) + full_bin.astype(
        jnp.float32
    )
    normed1, inverse1, pre1 = layer_stats(hidden_one, g1_f, e1_f)
    act_one = smooth_act(pre1).astype(jnp.bfloat16).reshape(seq_local, block_rows, inner)
    halo_rows = shifted(act_one[:, block_rows - 4 :], "ctx", 1)
    extended = jnp.concatenate([halo_rows, act_one], axis=1)
    tap_masks = []
    pieces = []
    for offset in range(3):
        begin_at = 4 - 2 * offset
        tap_mask = (seg_ext[:, begin_at : begin_at + block_rows] == own_segs).astype(jnp.float32)
        tap_masks.append(tap_mask)
        pieces.append(
            extended[:, begin_at : begin_at + block_rows]
            * tap_mask[:, :, None].astype(jnp.bfloat16)
        )
    stacked = jnp.concatenate(pieces, axis=-1).reshape(row_count, 3 * inner)
    hidden_two = jnp.dot(
        stacked, conv_flat, preferred_element_type=jnp.float32
    ) + full_bconv.astype(jnp.float32)
    normed2, inverse2, pre2 = layer_stats(hidden_two, g2_f, e2_f)
    act_two = smooth_act(pre2).astype(jnp.bfloat16)
    branch_out = jnp.dot(act_two, full_wout, preferred_element_type=jnp.float32) + full_bout.astype(
        jnp.float32
    )
    result = flat_rows + branch_out
    output = result.astype(jnp.bfloat16).reshape(seq_local, block_rows, wide_dim)
    local_squares = jnp.stack(
        [
            jnp.sum(flat_rows * flat_rows),
            jnp.sum(result * result),
            jnp.sum(hidden_one * hidden_one),
            jnp.sum(hidden_two * hidden_two),
            jnp.sum(branch_out * branch_out),
        ]
    )
    grad_out = cotangent.reshape(row_count, wide_dim)
    grad_out_f = grad_out.astype(jnp.float32)
    grad_bias_out = jnp.sum(grad_out_f, axis=0)
    grad_weight_out = jnp.einsum("rd,rw->dw", act_two, grad_out, preferred_element_type=jnp.float32)
    grad_act_two = jnp.einsum("rw,dw->rd", grad_out, full_wout, preferred_element_type=jnp.float32)
    grad_h2, grad_g2, grad_e2 = norm_back(grad_act_two, normed2, inverse2, pre2, g2_f)
    grad_h2 = grad_h2.astype(jnp.bfloat16)
    grad_bias_conv = jnp.sum(grad_h2.astype(jnp.float32), axis=0)
    grad_weight_conv = jnp.einsum(
        "rk,rd->kd", stacked, grad_h2, preferred_element_type=jnp.float32
    ).reshape(3, inner, inner)
    grad_stacked = jnp.einsum(
        "rd,kd->rk", grad_h2, conv_flat, preferred_element_type=jnp.float32
    ).reshape(seq_local, block_rows, 3, inner)
    grad_ext = jnp.zeros((seq_local, block_rows + 4, inner), jnp.float32)
    for offset in range(3):
        begin_at = 4 - 2 * offset
        piece_grad = grad_stacked[:, :, offset, :] * tap_masks[offset][:, :, None]
        grad_ext = grad_ext + jnp.pad(piece_grad, ((0, 0), (begin_at, 2 * offset), (0, 0)))
    back_rows = shifted(grad_ext[:, :4], "ctx", -1)
    grad_act_one = grad_ext[:, 4:] + jnp.pad(back_rows, ((0, 0), (block_rows - 4, 0), (0, 0)))
    grad_h1, grad_g1, grad_e1 = norm_back(
        grad_act_one.reshape(row_count, inner), normed1, inverse1, pre1, g1_f
    )
    grad_h1 = grad_h1.astype(jnp.bfloat16)
    grad_bias_in = jnp.sum(grad_h1.astype(jnp.float32), axis=0)
    grad_weight_in = jnp.einsum("rw,rd->wd", act_zero, grad_h1, preferred_element_type=jnp.float32)
    grad_act_zero = jnp.einsum("rd,wd->rw", grad_h1, full_win, preferred_element_type=jnp.float32)
    grad_x_branch, grad_g0, grad_e0 = norm_back(grad_act_zero, normed0, inverse0, pre0, g0_f)
    grad_stream = (
        (grad_out_f + grad_x_branch).astype(jnp.bfloat16).reshape(seq_local, block_rows, wide_dim)
    )
    dp_count = lax.axis_size("dp")
    extra_sums = jnp.zeros((dp_count, 5), jnp.float32)
    grad_terms = (
        grad_g0,
        grad_e0,
        grad_weight_in,
        grad_bias_in,
        grad_g1,
        grad_e1,
        grad_weight_conv,
        grad_bias_conv,
        grad_g2,
        grad_e2,
        grad_weight_out,
        grad_bias_out,
        extra_sums,
    )
    whole_sums = lax.psum(
        (
            grad_terms[0],
            grad_terms[1],
            grad_terms[2],
            grad_terms[3],
            grad_terms[4],
            grad_terms[5],
            grad_terms[6],
            grad_terms[7],
            grad_terms[8],
            grad_terms[9],
            grad_terms[10],
            grad_terms[11],
            grad_terms[12],
        ),
        "ctx",
    )
    summed = (
        lax.psum_scatter(whole_sums[0], "dp", scatter_dimension=0, tiled=True),
        lax.psum_scatter(whole_sums[1], "dp", scatter_dimension=0, tiled=True),
        lax.psum_scatter(whole_sums[2], "dp", scatter_dimension=0, tiled=True),
        lax.psum_scatter(whole_sums[3], "dp", scatter_dimension=0, tiled=True),
        lax.psum_scatter(whole_sums[4], "dp", scatter_dimension=0, tiled=True),
        lax.psum_scatter(whole_sums[5], "dp", scatter_dimension=0, tiled=True),
        lax.psum_scatter(whole_sums[6], "dp", scatter_dimension=1, tiled=True),
        lax.psum_scatter(whole_sums[7], "dp", scatter_dimension=0, tiled=True),
        lax.psum_scatter(whole_sums[8], "dp", scatter_dimension=0, tiled=True),
        lax.psum_scatter(whole_sums[9], "dp", scatter_dimension=0, tiled=True),
        lax.psum_scatter(whole_sums[10], "dp", scatter_dimension=0, tiled=True),
        lax.psum_scatter(whole_sums[11], "dp", scatter_dimension=0, tiled=True),
        lax.psum_scatter(whole_sums[12], "dp", scatter_dimension=0, tiled=True),
    )
    totals = lax.psum(local_squares, ("dp", "ctx"))
    position_count = row_count * dp_count * lax.axis_size("ctx")
    entry_wide = float(position_count * wide_dim)
    entry_inner = float(position_count * inner)
    rms_in = jnp.sqrt(totals[0] / entry_wide)
    rms_out = jnp.sqrt(totals[1] / entry_wide)
    rms_hidden_one = jnp.sqrt(totals[2] / entry_inner)
    rms_hidden_two = jnp.sqrt(totals[3] / entry_inner)
    rms_branch = jnp.sqrt(totals[4] / entry_wide)
    return (
        output,
        grad_stream,
        summed[0],
        summed[1],
        summed[2],
        summed[3],
        summed[4],
        summed[5],
        summed[6],
        summed[7],
        summed[8],
        summed[9],
        summed[10],
        summed[11],
        rms_in,
        rms_out,
        rms_hidden_one,
        rms_hidden_two,
        rms_branch,
    )


def solution(mesh):
    placed = (
        P("dp", "ctx", None),
        P("dp", None),
        P("dp", "ctx", None),
        P("dp"),
        P("dp"),
        P("dp", None),
        P("dp"),
        P("dp"),
        P("dp"),
        P(None, "dp", None),
        P("dp"),
        P("dp"),
        P("dp"),
        P("dp", None),
        P("dp"),
    )
    return jax.shard_map(
        local,
        mesh=mesh,
        in_specs=placed,
        out_specs=(
            P("dp", "ctx", None),
            P("dp", "ctx", None),
            P("dp"),
            P("dp"),
            P("dp", None),
            P("dp"),
            P("dp"),
            P("dp"),
            P(None, "dp", None),
            P("dp"),
            P("dp"),
            P("dp"),
            P("dp", None),
            P("dp"),
            P(),
            P(),
            P(),
            P(),
            P(),
        ),
        check_vma=False,
    )
```

profile of v0, /device:TPU:0, one launch (start us, length us, event | category | flops | bytes accessed | tf_op | source)
XLA Modules:
  0.0 575.2 jit_solution(186431466247948656)
XLA Ops:
  9.5 7.0 %fusion.2 = (f32[]{:T(128)}, f32[4,512]{1,0:T(4,128)S(1)}) fusion(bf16[4,512,1600]{1,2,0:T(8,128)(2,1)} %param.15), kind=kLoop, calls=%fused_computation.6 | loop fusion | flops 13105151 | bytes 6561796 | tf_op jit(solution)/shard_map/reduce_sum | solution.py:131
  16.6 6.9 %convert_bitcast_fusion = f32[4,200,8,512]{3,2,1,0:T(8,128)} fusion(bf16[4,512,1600]{1,2,0:T(8,128)(2,1)S(1)} %copy-done.3), kind=kLoop, calls=%fused_computation.3 | loop fusion | flops 3276800 | bytes 19660800
  27.5 19.0 %all-reduce.27 = (bf16[800]{0:T(1024)(128)(2,1)S(1)}, bf16[800]{0:T(1024)(128)(2,1)S(1)}, bf16[800]{0:T(1024)(128)(2,1)S(1)}, bf16[800]{0:T(1024)(128)(2,1)S(1)}...) all-reduce(bf16[800]{0:T(1024)(128)(2,1)S(1)} %dynamic-update-slice, ...), channel_id=1, replica_groups=mesh['dp'=4,'ctx'=8] {'dp'}, use_global_device_ids=true, to_apply=%add.11 | all-reduce | flops 9600 | bytes 38400
  46.7 4.6 fusion.1
  51.3 11.8 %copy.62 = f32[4,200,8,512]{3,2,0,1:T(8,128)} copy(f32[4,200,8,512]{3,2,1,0:T(8,128)} %convert_bitcast_fusion) | data formatting | bytes 26214400 | tf_op jit(solution)/shard_map/convert_element_type | solution.py:98
  63.1 11.2 %multiply_convert_fusion = bf16[2048,1600]{0,1:T(8,128)(2,1)} fusion(f32[2048,1600]{0,1:T(8,128)} %bitcast.86, f32[1600]{0:T(1024)S(1)} %convert_element_type.97, f32[1600]{0:T(1024)S(1)} %convert_element_type.96, f32[2048]{0:T(1024)S(1)} %bitcast.115, f32[2048]{0:T(1024)S(1)} %bitcast.111), kind=kLoop, calls=%fused_computation.14 | loop fusion | flops 29491200 | bytes 19689984 | tf_op jit(solution)/shard_map/convert_element_type | solution.py:100
  74.3 9.5 %add_reduce_fusion.1 = (f32[2048]{0:T(1024)S(1)}, f32[2048,800]{0,1:T(8,128)S(1)}) fusion(f32[800]{0:T(1024)S(1)} %convert_element_type.99, bf16[2048,1600]{0,1:T(8,128)(2,1)} %multiply_convert_fusion, bf16[1600,800]{1,0:T(8,128)(2,1)} %all-gather.4.cloned.1.call-done), kind=kOutput, calls=%fused_computation.56 | convolution fusion | flops 5246154752 | bytes 15678592 | tf_op jit(solution)/shard_map/dot_general | solution.py:101
  99.8 6.7 %copy.63 = bf16[4,200,8,512]{3,2,0,1:T(8,128)(2,1)} copy(bf16[4,200,8,512]{3,2,1,0:T(8,128)(2,1)} %bitcast.96) | data formatting | bytes 13107200 | tf_op jit(solution)/shard_map/reshape | solution.py:138
  107.8 10.0 %fusion.9 = (bf16[4,512,800]{1,0,2:T(4,128)(2,1)S(1)}, bf16[4,512,800]{1,0,2:T(4,128)(2,1)S(1)}) fusion(bf16[4,4,800]{1,0,2:T(4,128)(2,1)} %copy.44, bf16[4,512,800]{1,0,2:T(4,128)(2,1)} %reshape.180, bf16[4,512]{1,0:T(4,128)(2,1)S(1)} %get-tuple-element.113, bf16[4,512]{1,0:T(4,128)(2,1)S(1)} %get-tuple-element.123), kind=kLoop, calls=%fused_computation.62 | loop fusion | flops 19660800 | bytes 9864192 | tf_op jit(solution)/shard_map/mul | solution.py:115
  123.4 12.6 %add_reduce_fusion = (f32[2048]{0:T(1024)S(1)}, f32[2048,800]{0,1:T(8,128)S(1)}) fusion(f32[800]{0:T(1024)S(1)} %convert_element_type.107, bf16[2400,800]{1,0:T(8,128)(2,1)} %bitcast.119, bf16[2048,800]{0,1:T(8,128)(2,1)} %bitcast.100, bf16[2048,800]{0,1:T(8,128)(2,1)} %bitcast.98, bf16[2048,800]{0,1:T(8,128)(2,1)S(1)} %multiply_convert_fusion.4), kind=kOutput, calls=%fused_computation.55 | convolution fusion | flops 7897085952 | bytes 20235392 | tf_op jit(solution)/shard_map/dot_general | solution.py:119
  139.7 12.5 %all-gather.8.cloned.1.call-done = bf16[800,1600]{1,0:T(8,128)(2,1)} async-done(((bf16[200,1600]{1,0:T(8,128)(2,1)}), bf16[800,1600]{1,0:T(8,128)(2,1)}) %all-gather.8.cloned.1.call-update) | async-done | bytes 2560016 | tf_op jit(solution)/shard_map/all_gather | solution.py:67
  152.2 14.6 %multiply_reduce_fusion.7 = (f32[800]{0:T(1024)}, f32[2048]{0:T(1024)S(1)}, f32[2048]{0:T(1024)S(1)}, f32[]{:T(128)}, f32[800]{0:T(1024)}, /*index=5*/f32[2048,800]{0,1:T(8,128)S(1)}) fusion(f32[2048]{0:T(1024)S(1)} %add_rsqrt_fusion, f32[2048]{0:T(1024)S(1)} %broadcast_multiply_fusion.6, f32[2048,800]{0,1:T(8,128)} %copy-done.4, ...), kind=kOutput, calls=%fused_computation.33 | convolution fusion | flops 5278918656 | bytes 22269572 | tf_op jit(solution)/shard_map/rw,dw->rd/dot_general | solution.py:142
  166.7 6.0 %convert_reduce_fusion.2 = (f32[800]{0:T(1024)}, bf16[2048,800]{0,1:T(8,128)(2,1)}, bf16[2048,800]{0,1:T(8,128)(2,1)S(1)}) fusion(f32[2048]{0:T(1024)S(1)} %get-tuple-element.139, f32[2048]{0:T(1024)S(1)} %add_rsqrt_fusion, f32[2048]{0:T(1024)S(1)} %broadcast_multiply_fusion.6, f32[2048,800]{0,1:T(8,128)S(1)} %copy-done.5, ...), kind=kLoop, calls=%fused_computation.34 | loop fusion | flops 29490400 | bytes 19706368 | tf_op jit(solution)/shard_map/reduce_sum | solution.py:145
  174.4 10.8 %fusion.29 = f32[800,1600]{1,0:T(8,128)} fusion(bf16[2048,800]{0,1:T(8,128)(2,1)S(1)} %get-tuple-element.120, bf16[2048,1600]{0,1:T(8,128)(2,1)} %bitcast.93), kind=kOutput, calls=%fused_computation.99 | convolution fusion | flops 5242880000 | bytes 14950400 | tf_op jit(solution)/shard_map/rd,rw->dw/dot_general | solution.py:141
  185.3 8.3 %dot_general.37 = bf16[4,512,800]{1,0,2:T(4,128)(2,1)} reshape(bf16[2048,800]{0,1:T(8,128)(2,1)} %get-tuple-element.109) | data formatting | bytes 6553600 | tf_op jit(solution)/shard_map/rd,kd->rk/dot_general | solution.py:149
  193.6 18.9 %fusion.6 = f32[4,512,3,800]{1,3,2,0:T(8,128)} fusion(bf16[3,800,800]{2,1,0:T(8,128)(2,1)} %all-gather.6.cloned.1.call-done, bf16[4,512,800,1]{1,0,2,3:T(4,128)(2,1)} %bitcast.110), kind=kOutput, calls=%fused_computation.57 | convolution fusion | flops 7864320000 | bytes 26777600 | tf_op jit(solution)/shard_map/rd,kd->rk/dot_general | solution.py:149
  212.5 6.3 %slice_bitcast_fusion.2 = f32[4,512,800]{1,2,0:T(8,128)} fusion(f32[4,512,3,800]{1,3,2,0:T(8,128)} %fusion.6), kind=kLoop, calls=%fused_computation.30 | loop fusion | bytes 13107200 | tf_op jit(solution)/shard_map/squeeze | solution.py:155
  218.8 12.2 %fusion.5 = (f32[4,512,800]{1,2,0:T(8,128)}, f32[4,512,800]{1,2,0:T(8,128)}) fusion(f32[4,512,3,800]{1,3,2,0:T(8,128)} %fusion.6, f32[4,512]{1,0:T(4,128)S(1)} %get-tuple-element.114, f32[4,512]{1,0:T(4,128)S(1)} %get-tuple-element.124), kind=kLoop, calls=%fused_computation.29 | loop fusion | flops 3276800 | bytes 26230784 | tf_op jit(solution)/shard_map/mul | solution.py:155
  238.0 11.2 %pad_add_fusion = f32[4,516,800]{1,2,0:T(8,128)} fusion(f32[4,512,800]{1,2,0:T(8,128)} %get-tuple-element.119, f32[4,512,800]{1,2,0:T(8,128)} %get-tuple-element.118, f32[4,512,800]{1,2,0:T(8,128)} %slice_bitcast_fusion.2), kind=kLoop, calls=%fused_computation.21 | loop fusion | flops 3302400 | bytes 26265600 | tf_op jit(solution)/shard_map/add | solution.py:156
  250.9 5.9 %fusion.3 = f32[4,100,8,512]{3,2,1,0:T(8,128)S(1)} fusion(f32[4,516,800]{1,2,0:T(8,128)} %pad_add_fusion, f32[4,4,800]{1,2,0:T(8,128)} %copy.50), kind=kLoop, calls=%fused_computation.25 | loop fusion | flops 1638400 | bytes 13158400
  257.9 10.1 %multiply_reduce_fusion.8 = (f32[800]{0:T(1024)S(1)}, f32[2048]{0:T(1024)S(1)}, f32[2048]{0:T(1024)S(1)}, f32[]{:T(128)}, f32[800]{0:T(1024)S(1)}, /*index=5*/f32[2048,800]{0,1:T(8,128)S(1)}) fusion(f32[2048]{0:T(1024)S(1)} %add_rsqrt_fusion.1, f32[2048]{0:T(1024)S(1)} %broadcast_multiply_fusion.7, f32[2048,800]{0,1:T(8,128)} %copy-done.2, ...), kind=kLoop, calls=%fused_computation.35 | loop fusion | flops 36039104 | bytes 19709572 | tf_op jit(solution)/shard_map/reduce_sum | solution.py:28
  272.7 9.0 %fusion.28 = f32[1600,800]{1,0:T(8,128)} fusion(bf16[2048,1600]{0,1:T(8,128)(2,1)S(1)} %bitcast.106, bf16[2048,800]{0,1:T(8,128)(2,1)S(1)} %get-tuple-element.111), kind=kOutput, calls=%fused_computation.98 | convolution fusion | flops 5242880000 | bytes 14950400 | tf_op jit(solution)/shard_map/rw,rd->wd/dot_general | solution.py:164
  286.1 12.7 %fusion.11 = f32[3,800,800]{2,1,0:T(8,128)} fusion(bf16[3,800,2048]{2,1,0:T(8,128)(2,1)S(1)} %bitcast.104, bf16[2048,800]{0,1:T(8,128)(2,1)S(1)} %copy-done.6), kind=kOutput, calls=%fused_computation.65 | convolution fusion | flops 7864320000 | bytes 20787200 | tf_op jit(solution)/shard_map/rk,rd->kd/dot_general | solution.py:146
  304.3 18.2 %add_multiply_fusion = f32[2048,1600]{0,1:T(8,128)} fusion(bf16[1600,800]{1,0:T(8,128)(2,1)} %all-gather.4.cloned.1.call-done, bf16[2048,800]{0,1:T(8,128)(2,1)} %copy-done.9, f32[2048,1600]{0,1:T(8,128)} %bitcast.87, f32[1600]{0:T(1024)S(1)} %copy-done.18, f32[1600]{0:T(1024)S(1)} %copy-done.12, f32[2048]{0:T(1024)S(1)} %bitcast.116, f32[2048]{0:T(1024)S(1)} %bitcast.112), kind=kOutput, calls=%fused_computation.13 | convolution fusion | flops 5282201600 | bytes 32080384 | tf_op jit(solution)/shard_map/rd,wd->rw/dot_general | solution.py:165
  322.4 23.0 %multiply_reduce_fusion = (f32[]{:T(128)}, f32[]{:T(128)}, f32[2048]{0:T(1024)S(1)}, f32[2048]{0:T(1024)S(1)}, f32[1600]{0:T(1024)S(1)}, /*index=5*/f32[1600]{0:T(1024)S(1)}, bf16[2048,1600]{0,1:T(8,128)(2,1)}) fusion(f32[1600]{0:T(1024)S(1)} %convert_element_type.111, f32[2048,1600]{0,1:T(8,128)} %bitcast.88, f32[2048,1600]{0,1:T(8,128)} %add_multiply_fusion, ...), kind=kOutput, calls=%fused_computation.7 | convolution fusion | flops 5295301632 | bytes 38663176 | tf_op jit(solution)/shard_map/dot_general | solution.py:124
  349.5 41.2 %psum.103 = f32[5]{0:T(128)S(1)} all-reduce(f32[5]{0:T(128)S(1)} %stack.23), channel_id=1, replica_groups=mesh['dp'=4,'ctx'=8] {'dp','ctx'}, use_global_device_ids=true, to_apply=%region_50.51 | all-reduce | flops 5 | bytes 40 | tf_op jit(solution)/shard_map/psum | solution.py:220
  394.8 46.5 %reduce-scatter.8.cloned.1.call-done = f32[3,200,800]{2,1,0:T(8,128)} async-done(((f32[3,800,800]{2,1,0:T(8,128)}), f32[3,200,800]{2,1,0:T(8,128)}) %reduce-scatter.8.cloned.1.call-update) | async-done | bytes 1920016 | tf_op jit(solution)/shard_map/reduce_scatter | solution.py:212
  441.3 12.8 %add_convert_fusion = bf16[2048,1600]{0,1:T(8,128)(2,1)S(1)} fusion(bf16[2048,1600]{0,1:T(8,128)(2,1)} %bitcast.94, f32[2048,1600]{0,1:T(8,128)} %add_multiply_fusion, f32[2048,1600]{0,1:T(8,128)} %bitcast.89, f32[2048]{0:T(1024)S(1)} %broadcast_multiply_fusion, f32[2048]{0:T(1024)S(1)} %broadcast_multiply_fusion.1, f32[1600]{0:T(1024)S(1)} %copy-done.12, ...), kind=kLoop, calls=%fused_computation.11 | loop fusion | flops 32768000 | bytes 39360768 | tf_op jit(solution)/shard_map/convert_element_type | solution.py:168
  457.5 15.7 %all-reduce.26 = (f32[1600]{0:T(1024)S(1)}, f32[1600]{0:T(1024)S(1)}, f32[800]{0:T(1024)S(1)}, f32[800]{0:T(1024)S(1)}, f32[800]{0:T(1024)S(1)}, /*index=5*/f32[...) all-reduce(f32[1600]{0:T(1024)S(1)} %get-tuple-element.68, ...), channel_id=2, replica_groups=mesh['dp'=4,'ctx'=8] {'dp'}, use_global_device_ids=true, to_apply=%region_14.0.clone | all-reduce | flops 9600 | bytes 76800
  473.9 6.4 %copy.74 = bf16[200,4,8,512]{3,2,0,1:T(8,128)(2,1)} copy(bf16[200,4,8,512]{3,2,1,0:T(8,128)(2,1)} %bitcast.107) | data formatting | bytes 13107200 | tf_op jit(solution)/shard_map/reshape | solution.py:128
  480.3 27.1 %all-reduce.24 = (f32[400]{0:T(512)}, f32[400]{0:T(512)}, f32[200]{0:T(256)}, f32[200]{0:T(256)}, f32[200]{0:T(256)}, /*index=5*/f32[200]{0:T(256)}, f32[200]{0:T(256)}, f32[200]{0:T(256)}, f32[400]{0:T(512)}) all-reduce(f32[400]{0:T(512)S(1)} %dynamic-slice.10, f32[400]{0:T(512)S(1)} %dynamic-slice.12, ...), channel_id=1, replica_groups=mesh['dp'=4,'ctx'=8] {'ctx'}, use_global_device_ids=true, to_apply=%region_13.0 | all-reduce | flops 2400 | bytes 19200 | tf_op jit(solution)/shard_map/psum | solution.py:187
  507.4 48.0 %all-reduce.30.cloned.1.call-done = (f32[400,800]{1,0:T(8,128)}, f32[3,200,800]{2,1,0:T(8,128)}, f32[200,1600]{1,0:T(8,128)}) async-done(((f32[400,800]{1,0:T(8,128)}, f32[3,200,800]{2,1,0:T(8,128)}, f32[200,1600]{1,0:T(8,128)}), (f32[400,800]{1,0:T(8,128)}, f32[3,200,800]{2,1,0:T(8,128)}, f32[200,1600]{1,0:T(8,128)})) %all-reduce.30.cloned.1.call-update) | async-done | bytes 4480016 | tf_op jit(solution)/shard_map/psum | solution.py:187
  (173 shorter events, 71.9 us)
Async XLA Ops:
  7.2 39.4 %copy-start = (s32[4,4096]{1,0:T(4,128)S(1)}, s32[4,4096]{1,0:T(4,128)}, u32[]{:S(2)}) copy-start(s32[4,4096]{1,0:T(4,128)} %param.16) | copy-start | bytes 196612
  7.2 67.1 %all-gather.4.cloned.1.call-start = ((), (), s32[]{:S(2)}) async-start(), calls=%async_computation.3 | async-start | bytes 3584000 | tf_op jit(solution)/shard_map/all_gather | solution.py:59
  7.9 115.4 %all-gather.6.cloned.1.call-start = ((), (), s32[]{:S(2)}) async-start(), calls=%async_computation.4 | async-start | bytes 5376000 | tf_op jit(solution)/shard_map/all_gather | solution.py:63
  8.7 143.5 %all-gather.8.cloned.1.call-start = ((), (), s32[]{:S(2)}) async-start(), calls=%async_computation.5 | async-start | bytes 3328000 | tf_op jit(solution)/shard_map/all_gather | solution.py:67
  9.4 385.3 %reduce-scatter.12.cloned.1.call-start = ((), (), s32[]{:S(2)}) async-start(), calls=%async_computation.8 | async-start | bytes 6656000
  9.5 7.0 %copy-start.3 = (bf16[4,512,1600]{1,2,0:T(8,128)(2,1)S(1)}, bf16[4,512,1600]{1,2,0:T(8,128)(2,1)}, u32[]{:S(2)}) copy-start(bf16[4,512,1600]{1,2,0:T(8,128)(2,1)} %param.15) | copy-start | bytes 19660804
  16.5 7.0 %copy-start.23 = (u32[32]{0:T(128)S(1)}, u32[32]{0:T(128)}, u32[]{:S(2)}) copy-start(u32[32]{0:T(128)} %constant.62) | copy-start | bytes 388
  16.5 8.9 %copy-start.27 = (bf16[200]{0:T(256)(128)(2,1)S(1)}, bf16[200]{0:T(256)(128)(2,1)}, u32[]{:S(2)}) copy-start(bf16[200]{0:T(256)(128)(2,1)} %param.21) | copy-start | bytes 1204
  16.5 9.1 %copy-start.28 = (bf16[200]{0:T(256)(128)(2,1)S(1)}, bf16[200]{0:T(256)(128)(2,1)}, u32[]{:S(2)}) copy-start(bf16[200]{0:T(256)(128)(2,1)} %param.22) | copy-start | bytes 1204
  16.5 9.3 %copy-start.29 = (bf16[200]{0:T(256)(128)(2,1)S(1)}, bf16[200]{0:T(256)(128)(2,1)}, u32[]{:S(2)}) copy-start(bf16[200]{0:T(256)(128)(2,1)} %param.23) | copy-start | bytes 1204
  16.5 9.6 %copy-start.30 = (bf16[200]{0:T(256)(128)(2,1)S(1)}, bf16[200]{0:T(256)(128)(2,1)}, u32[]{:S(2)}) copy-start(bf16[200]{0:T(256)(128)(2,1)} %param.26) | copy-start | bytes 1204
  16.5 9.8 %copy-start.31 = (bf16[200]{0:T(256)(128)(2,1)S(1)}, bf16[200]{0:T(256)(128)(2,1)}, u32[]{:S(2)}) copy-start(bf16[200]{0:T(256)(128)(2,1)} %param.27) | copy-start | bytes 1204
  16.5 10.0 %copy-start.32 = (bf16[200]{0:T(256)(128)(2,1)S(1)}, bf16[200]{0:T(256)(128)(2,1)}, u32[]{:S(2)}) copy-start(bf16[200]{0:T(256)(128)(2,1)} %param.25) | copy-start | bytes 1204
  16.5 10.2 %copy-start.24 = (bf16[400]{0:T(512)(128)(2,1)S(1)}, bf16[400]{0:T(512)(128)(2,1)}, u32[]{:S(2)}) copy-start(bf16[400]{0:T(512)(128)(2,1)} %param.18) | copy-start | bytes 2404
  16.6 10.5 %copy-start.25 = (bf16[400]{0:T(512)(128)(2,1)S(1)}, bf16[400]{0:T(512)(128)(2,1)}, u32[]{:S(2)}) copy-start(bf16[400]{0:T(512)(128)(2,1)} %param.19) | copy-start | bytes 2404
  16.6 10.7 %copy-start.26 = (bf16[400]{0:T(512)(128)(2,1)S(1)}, bf16[400]{0:T(512)(128)(2,1)}, u32[]{:S(2)}) copy-start(bf16[400]{0:T(512)(128)(2,1)} %param.29) | copy-start | bytes 2404
  46.7 16.5 %copy-start.11 = (f32[1600]{0:T(1024)}, f32[1600]{0:T(1024)S(1)}, u32[]{:S(2)}) copy-start(f32[1600]{0:T(1024)S(1)} %convert_element_type.96) | copy-start | bytes 19204
  46.7 16.5 %copy-start.17 = (f32[1600]{0:T(1024)}, f32[1600]{0:T(1024)S(1)}, u32[]{:S(2)}) copy-start(f32[1600]{0:T(1024)S(1)} %convert_element_type.97) | copy-start | bytes 19204
  46.7 16.4 %copy-start.13 = (f32[1,4,4,128]{3,1,2,0:T(4,128)}, f32[1,4,4,128]{3,1,2,0:T(4,128)S(1)}, u32[]{:S(2)}) copy-start(f32[1,4,4,128]{3,1,2,0:T(4,128)S(1)} %copy.65) | copy-start | bytes 24580
  51.3 11.8 %copy-start.15 = (f32[1,4,4,128]{3,1,2,0:T(4,128)}, f32[1,4,4,128]{3,1,2,0:T(4,128)S(1)}, u32[]{:S(2)}) copy-start(f32[1,4,4,128]{3,1,2,0:T(4,128)S(1)} %copy.66) | copy-start | bytes 24580
  98.4 8.1 %collective-permute-start = (bf16[4,4,800]{2,1,0:T(4,128)(2,1)S(1)}, bf16[4,4,800]{2,1,0:T(4,128)(2,1)S(1)}, u32[]{:S(2)}, u32[]{:S(2)}) collective-permute-start(bf16[4,4,800]{2,1,0:T(4,128)(2,1)S(1)} %copy.57), channel_id=1, source_target_pairs={{0,1},{1,2},{2,3},{3,4},{4,5},{5,6},{6,7},{8,9},{9,10},{10,11},{11... | collective-permute-start | bytes 76808 | tf_op jit(solution)/shard_map/ppermute | solution.py:10
  152.2 14.6 %copy-start.5 = (f32[2048,800]{0,1:T(8,128)S(1)}, f32[2048,800]{0,1:T(8,128)}, u32[]{:S(2)}) copy-start(f32[2048,800]{0,1:T(8,128)} %copy-done.4) | copy-start | bytes 19660804
  185.3 209.5 %reduce-scatter.10.cloned.1.call-start = ((), (), s32[]{:S(2)}) async-start(), calls=%async_computation.7 | async-start | bytes 7168000
  236.7 12.5 %collective-permute-start.1 = (f32[4,4,800]{2,1,0:T(4,128)S(1)}, f32[4,4,800]{2,1,0:T(4,128)S(1)}, u32[]{:S(2)}, u32[]{:S(2)}) collective-permute-start(f32[4,4,800]{2,1,0:T(4,128)S(1)} %copy.49), channel_id=1, source_target_pairs={{1,0},{2,1},{3,2},{4,3},{5,4},{6,5},{7,6},{9,8},{10,9},{11,10},{12... | collective-permute-start | bytes 153608 | tf_op jit(solution)/shard_map/ppermute | solution.py:10
  256.8 11.2 %slice-start = ((s8[6553600]{0:T(1024)(128)(4,1)}), s8[2359296]{0:T(1024)(128)(4,1)S(1)}, s32[]{:S(2)}) async-start(s8[6553600]{0:T(1024)(128)(4,1)} %bitcast.90), calls=%async_computation.10 | async-start | bytes 4718592
  256.8 15.9 %slice-start.2 = ((s8[6553600]{0:T(1024)(128)(4,1)}), s8[4194304]{0:T(1024)(128)(4,1)S(1)}, s32[]{:S(2)}) async-start(s8[6553600]{0:T(1024)(128)(4,1)} %bitcast.105), calls=%async_computation.12 | async-start | bytes 8388608
  257.9 10.1 %slice-start.1 = ((s8[6553600]{0:T(1024)(128)(4,1)}), s8[4194304]{0:T(1024)(128)(4,1)S(1)}, s32[]{:S(2)}) async-start(s8[6553600]{0:T(1024)(128)(4,1)} %bitcast.90), calls=%async_computation.11 | async-start | bytes 8388608
  257.9 14.7 %slice-start.3 = ((s8[6553600]{0:T(1024)(128)(4,1)}), s8[2359296]{0:T(1024)(128)(4,1)S(1)}, s32[]{:S(2)}) async-start(s8[6553600]{0:T(1024)(128)(4,1)} %bitcast.105), calls=%async_computation.13 | async-start | bytes 4718592
  281.7 159.6 %reduce-scatter.8.cloned.1.call-start = ((), (), s32[]{:S(2)}) async-start(), calls=%async_computation.6 | async-start | bytes 10752000 | tf_op jit(solution)/shard_map/reduce_scatter | solution.py:212
  298.8 256.6 %all-reduce.30.cloned.1.call-start = ((), (), s32[]{:S(2)}) async-start(), calls=%async_computation.9 | async-start | bytes 9830400 | tf_op jit(solution)/shard_map/psum | solution.py:187
  304.3 18.2 %copy-start.8 = (bf16[2048,800]{0,1:T(8,128)(2,1)S(1)}, bf16[2048,800]{0,1:T(8,128)(2,1)}, u32[]{:S(2)}) copy-start(bf16[2048,800]{0,1:T(8,128)(2,1)} %copy-done.7) | copy-start | bytes 9830404
  473.9 88.3 %copy-start.1 = (s32[4,4096]{1,0:T(4,128)S(1)}, s32[4,4096]{1,0:T(4,128)}, u32[]{:S(2)}) copy-start(s32[4,4096]{1,0:T(4,128)} %param.16) | copy-start | bytes 196612
  (14 other events, 51.8 us)
Sparse Core Ops, SparseCore 0:
  9.9 44.7 all-gather.3
  56.5 53.7 all-gather.5
  112.1 39.9 all-gather.7
  185.4 63.8 reduce-scatter.11
  281.8 67.0 reduce-scatter.9
  351.8 89.4 reduce-scatter.7
  444.1 111.2 all-reduce.29
where the time goes:
time: 581 us; the launch traced here: 575 us
  matrix products  129 us (22%)
  other arithmetic  118 us (20%)
  waiting for transfers between devices  109 us (19%)
  blocking collectives  103 us (18%)
  local copies, waits for them, and re-layouts  86 us (15%)
  between operations  26.9 us (5%)
    psum x1, waiting for transfers between devices, local(): lax.psum((grad_terms[0], grad_terms[1], grad_terms[2], grad_terms[3], gra...  48 us
    reduce_scatter x1, waiting for transfers between devices, local(): lax.psum_scatter(whole_sums[6], 'dp', scatter_dimension=1, tiled=True)  46.5 us
    psum x1, blocking collectives, local(): totals = lax.psum(local_squares, ('dp', 'ctx'))  41.2 us
    unnamed x2, blocking collectives  34.8 us
    psum x1, blocking collectives, local(): lax.psum((grad_terms[0], grad_terms[1], grad_terms[2], grad_terms[3], gra...  27.1 us
    unnamed x110, local copies, waits for them, and re-layouts  26.4 us
    dot_general x1, matrix products, local(): jnp.dot(act_two, full_wout, preferred_element_type=jnp.float32)  23 us
    dot_general x1, matrix products, local(): jnp.einsum('rd,kd->rk', grad_h2, conv_flat, preferred_element_type=jnp.fl...  18.9 us
  transfers between devices with their start and end apart: 9, of which 3 were waited for; matrix products, arithmetic and copies ran while one was open for 50% of the time, Pallas kernels for 0%

commit v1 on v0

v1 whole, which is shorter than its diff:
```python
import jax
import jax.numpy as jnp
from jax import lax
from jax.experimental import pallas as pl
from jax.experimental.pallas import tpu as pltpu
from jax.sharding import PartitionSpec as P

F32 = jnp.float32
BF = jnp.bfloat16
EPS = 1e-05
ROWS = 16
NN = (((1,), (0,)), ((), ()))
NT = (((1,), (1,)), ((), ()))
MIB = 1024 * 1024


def by_core(value, even_mask, odd_mask):
    n_dp, n_ctx = lax.axis_size("dp"), lax.axis_size("ctx")
    masks = (even_mask, odd_mask)
    pairs = [
        (d * n_ctx + t, (d ^ masks[t % 2]) * n_ctx + t) for d in range(n_dp) for t in range(n_ctx)
    ]
    return lax.ppermute(value, ("dp", "ctx"), pairs)


def swap(value, axis, mask):
    return lax.ppermute(value, axis, [(i, i ^ mask) for i in range(lax.axis_size(axis))])


def shifted(value, by):
    size = lax.axis_size("ctx")
    return lax.ppermute(value, "ctx", [(i, i + by) for i in range(size) if 0 <= i + by < size])


def half_of(rows):
    off = rows // 2 // 16 * 16
    return off, rows - off


def gather_pieces(shard, row_dim, core):
    off, size = half_of(shard.shape[row_dim])
    own_half = lax.dynamic_slice_in_dim(shard, core * off, size, row_dim)
    first = by_core(own_half, 1, 2)
    second = by_core(jnp.stack([own_half, first]), 2, 1)
    other_first = swap(first, "ctx", 1)
    other_second = swap(second, "ctx", 1)
    return shard, first, second, other_first, other_second


def sum_shards(keep, send):
    from_core = swap(send, "ctx", 1).astype(F32)
    one = by_core((keep[2:4] + from_core[2:4]).astype(BF), 1, 2).astype(F32)
    two = by_core((keep[1] + from_core[1] + one[1]).astype(BF), 2, 1).astype(F32)
    part = keep[0] + from_core[0] + one[0] + two
    mask = 2
    while mask < lax.axis_size("ctx"):
        part = part.astype(BF)
        part = part.astype(F32) + swap(part, "ctx", mask).astype(F32)
        mask *= 2
    return part, swap(part, "ctx", 1)


def join_halves(mine, other, rows, row_dim, core):
    off, size = half_of(rows)
    low = jnp.where(core == 0, mine, other)
    high = jnp.where(core == 0, other, mine)
    return jnp.concatenate(
        [low, lax.slice_in_dim(high, size - off, size, axis=row_dim)], axis=row_dim
    )


def sum_all(value):
    value = value + swap(value, "ctx", 1)
    value = value + swap(value, "dp", 1)
    value = value + swap(value, "dp", 2)
    mask = 2
    while mask < lax.axis_size("ctx"):
        value = value + swap(value, "ctx", mask)
        mask *= 2
    return value


def mm(left, right, dims=NN):
    return lax.dot_general(left, right, dims, preferred_element_type=F32)


def sig(z):
    return 0.5 * jnp.tanh(0.5 * z) + 0.5


def loop(count, body, unroll):
    lax.fori_loop(0, count, lambda i, _: (body(i), 0)[1], 0, unroll=unroll)


def full(shape):
    return pl.BlockSpec(shape, lambda s: (0,) * len(shape), pipeline_mode=pl.Buffered(1))


def seq(shape):
    return pl.BlockSpec((None,) + shape, lambda s: (s,) + (0,) * len(shape))


ANY = pl.BlockSpec(memory_space=pl.ANY)


def sds(shape, dtype):
    return jax.ShapeDtypeStruct(shape, dtype)


def rows_at(i, base=0):
    return pl.ds(pl.multiple_of(i * ROWS + base, ROWS), ROWS)


def lanes(tile, width):
    return jnp.concatenate([tile] * (width // 128), axis=1)


def col(ref, j, r, width):
    return lanes(ref[j, r, :], width)


def fold(v):
    t = v[:, 0:128]
    for j in range(1, v.shape[1] // 128):
        t = t + v[:, j * 128 : (j + 1) * 128]
    return t


def eight(v):
    return v[0:8] + v[8:16]


def spread(vec_ref, out_ref, j, row):
    v = vec_ref[row : row + 1, :]
    out_ref[j] = jnp.broadcast_to(v, (128, v.shape[1])).T


def gathered_row(sums):
    return jnp.sum(sums.T, axis=0, keepdims=True)


def row_stats(count, load, width, length):
    def total(i, a):
        return a + eight(load(i))

    zero = jnp.zeros((8, length), F32)
    a = lax.fori_loop(0, count, total, zero, unroll=5)
    mean = jnp.sum(a, axis=0, keepdims=True) * (1.0 / width)

    def squares(i, a):
        c = load(i) - mean
        return a + eight(c * c)

    a = lax.fori_loop(0, count, squares, zero, unroll=5)
    var = jnp.sum(a, axis=0, keepdims=True) * (1.0 / width)
    return mean, var


def start_load(pieces, dst, sems):
    shard, first, second, other_first, other_second = pieces
    rows = shard.shape[0]
    off, size = half_of(rows)
    me, core = lax.axis_index("dp"), lax.rem(lax.axis_index("ctx"), 2)
    near = jnp.bitwise_xor(me, 1 + core)
    far = jnp.bitwise_xor(me, 2 - core)
    both = jnp.bitwise_xor(me, 3)

    def at(device, half, count):
        return dst.at[pl.ds(pl.multiple_of(device * rows + half * off, 16), count), :]

    batch_one = [
        (shard, at(me, 0, rows)),
        (first, at(near, core, size)),
        (second.at[0], at(far, core, size)),
        (second.at[1], at(both, core, size)),
    ]
    batch_two = [
        (other_first, at(far, 1 - core, size)),
        (other_second.at[0], at(near, 1 - core, size)),
        (other_second.at[1], at(both, 1 - core, size)),
    ]
    copies = [
        pltpu.make_async_copy(src, to, sems.at[i])
        for i, (src, to) in enumerate(batch_one + batch_two)
    ]
    for c in copies[:4]:
        c.start()
    return copies


def finish_load(copies):
    for c in copies[:4]:
        c.wait()
    for c in copies[4:]:
        c.start()
    for c in copies[4:]:
        c.wait()


def assemble(pieces, wide_s):
    shard, first, second, other_first, other_second = pieces
    rows = shard.shape[0]
    off, size = half_of(rows)
    me, core = lax.axis_index("dp"), lax.rem(lax.axis_index("ctx"), 2)
    near = jnp.bitwise_xor(me, 1 + core)
    far = jnp.bitwise_xor(me, 2 - core)
    both = jnp.bitwise_xor(me, 3)

    def put(device, half, piece):
        start = pl.ds(pl.multiple_of(device * rows + half * off, 8), piece.shape[0])
        wide_s[start, :] = piece.astype(F32)

    put(me, 0, shard[...])
    put(near, core, first[...])
    put(far, core, second[0])
    put(both, core, second[1])
    put(far, 1 - core, other_first[...])
    put(near, 1 - core, other_second[0])
    put(both, 1 - core, other_second[1])
    return wide_s[...].astype(BF)


def params(mib):
    return pltpu.CompilerParams(vmem_limit_bytes=mib * MIB)


def split_grad(acc_ref, keep_ref, send_ref, lead):
    me, core = lax.axis_index("dp"), lax.rem(lax.axis_index("ctx"), 2)
    rows = acc_ref.shape[lead] // 4
    off, size = half_of(rows)
    mine = (0, 2 - core, 1 + core, 3)
    theirs = (0, 1 + core, 2 - core, 3)
    for j in range(4):
        a = pl.ds(pl.multiple_of(jnp.bitwise_xor(me, mine[j]) * rows + core * off, 8), size)
        b = pl.ds(pl.multiple_of(jnp.bitwise_xor(me, theirs[j]) * rows + (1 - core) * off, 8), size)
        if lead:
            for k in range(acc_ref.shape[0]):
                keep_ref[j, k] = acc_ref[k, a, :]
                send_ref[j, k] = acc_ref[k, b, :].astype(BF)
        else:
            keep_ref[j] = acc_ref[a, :]
            send_ref[j] = acc_ref[b, :].astype(BF)


def first_body(
    x_ref, p0, p1, p2, p3, p4, vw_ref, vi_ref,
    a0_ref, h1_ref, a1_ref, edge_ref, sq_ref,
    w_s, wt_s, vw_s, vi_s, sems,
):
    s = pl.program_id(0)
    wide, length = x_ref.shape
    inner = h1_ref.shape[0]

    @pl.when(s == 0)
    def _():
        copies = start_load((p0, p1, p2, p3, p4), w_s, sems)
        sq_ref[...] = jnp.zeros_like(sq_ref)
        for j in range(2):
            spread(vw_ref, vw_s, j, j)
        for j in range(3):
            spread(vi_ref, vi_s, j, j)
        finish_load(copies)
        wt_s[...] = w_s[...].T

    mean, var = row_stats(wide // ROWS, lambda i: x_ref[rows_at(i), :].astype(F32), wide, length)
    inv = lax.rsqrt(var + EPS)
    sq_ref[0:1, :] += (var + mean * mean) * float(wide)

    def act0(i):
        r = rows_at(i)
        z = (x_ref[r, :].astype(F32) - mean) * inv * col(vw_s, 0, r, length)
        z = z + col(vw_s, 1, r, length)
        a0_ref[r, :] = (z * sig(z)).astype(BF)

    loop(wide // ROWS, act0, 5)
    h1_ref[...] = mm(wt_s[...], a0_ref[...]) + lanes(vi_s[0], length)
    mean1, var1 = row_stats(inner // ROWS, lambda i: h1_ref[rows_at(i), :], inner, length)
    inv1 = lax.rsqrt(var1 + EPS)
    sq_ref[1:2, :] += (var1 + mean1 * mean1) * float(inner)

    def act1(i):
        r = rows_at(i)
        z = (h1_ref[r, :] - mean1) * inv1 * col(vi_s, 1, r, length) + col(vi_s, 2, r, length)
        a1_ref[r, :] = (z * sig(z)).astype(BF)

    loop(inner // ROWS, act1, 5)
    edge_ref[...] = a1_ref[:, length - 128 :].astype(F32).T[120:128, :].astype(BF)


def first(x, pieces, vw, vi):
    seqs, wide, length = x.shape
    inner = pieces[0].shape[1]
    return pl.pallas_call(
        first_body,
        grid=(seqs,),
        in_specs=[seq((wide, length))] + [ANY] * 5 + [full(vw.shape), full(vi.shape)],
        out_specs=[
            seq((wide, length)),
            seq((inner, length)),
            seq((inner, length)),
            seq((8, inner)),
            full((8, length)),
        ],
        out_shape=[
            sds((seqs, wide, length), BF),
            sds((seqs, inner, length), F32),
            sds((seqs, inner, length), BF),
            sds((seqs, 8, inner), BF),
            sds((8, length), F32),
        ],
        scratch_shapes=[
            pltpu.VMEM((wide, inner), BF),
            pltpu.VMEM((inner, wide), BF),
            pltpu.VMEM((2, wide, 128), F32),
            pltpu.VMEM((3, inner, 128), F32),
            pltpu.SemaphoreType.DMA((7,)),
        ],
        compiler_params=params(40),
        name="norm_and_first_product",
    )(x, *pieces, vw, vi)


def conv_body(
    a1_ref, halo_ref, dy_ref, mk_ref, c0, c1, c2, c3, c4, o0, o1, o2, o3, o4, vi_ref,
    a2_ref, dh2_ref, edge_ref, sums_ref, bo_ref, sq_ref, wc_ref, wot_ref,
    wct_s, wo_s, st_s, h_s, d_s, hl_s, vi_s, sums_s, bo_s, tap_s, out_s,
):
    s = pl.program_id(0)
    inner, length = a1_ref.shape
    wide = dy_ref.shape[0]
    steps = inner // ROWS

    @pl.when(s == 0)
    def _():
        sq_ref[...] = jnp.zeros_like(sq_ref)
        sums_s[...] = jnp.zeros_like(sums_s)
        bo_s[...] = jnp.zeros_like(bo_s)
        for j in range(3):
            spread(vi_ref, vi_s, j, j + 3)
        for k in range(3):
            wc_ref[k] = assemble(
                (c0.at[k], c1.at[k], c2.at[:, k], c3.at[k], c4.at[:, k]), tap_s
            )
        wct_s[...] = wc_ref[...].reshape(3 * inner, inner).T
        wo_s[...] = assemble((o0, o1, o2, o3, o4), out_s)
        wot_ref[...] = wo_s[...].T

    hl_s[...] = jnp.concatenate(
        [jnp.zeros((120, inner), F32), halo_ref[...].astype(F32)], axis=0
    ).T
    m1 = mk_ref[1:2, :]
    m2 = mk_ref[2:3, :]

    def build(i):
        r = rows_at(i)
        b = a1_ref[r, :]
        v = jnp.concatenate([b.astype(F32), hl_s[r, :]], axis=1)
        st_s[r, :] = b
        st_s[rows_at(i, inner), :] = (pltpu.roll(v, 2, 1)[:, 0:length] * m1).astype(BF)
        st_s[rows_at(i, 2 * inner), :] = (pltpu.roll(v, 4, 1)[:, 0:length] * m2).astype(BF)

    loop(steps, build, 2)
    h_s[...] = mm(wct_s[...], st_s[...]) + lanes(vi_s[0], length)
    d_s[...] = mm(wo_s[...], dy_ref[...])
    mean, var = row_stats(steps, lambda i: h_s[rows_at(i), :], inner, length)
    inv = lax.rsqrt(var + EPS)
    sq_ref[0:1, :] += (var + mean * mean) * float(inner)

    def back(i, acc):
        r = rows_at(i)
        n = (h_s[r, :] - mean) * inv
        g = col(vi_s, 1, r, length)
        z = n * g + col(vi_s, 2, r, length)
        sg = sig(z)
        zs = z * sg
        a2_ref[r, :] = zs.astype(BF)
        e = d_s[r, :] * (sg + zs * (1.0 - sg))
        q = e * g
        d_s[r, :] = q
        h_s[r, :] = n
        sums_s[0, r, :] += fold(e * n)
        sums_s[1, r, :] += fold(e)
        return acc[0] + eight(q), acc[1] + eight(q * n)

    zero = jnp.zeros((8, length), F32)
    qa, qn = lax.fori_loop(0, steps, back, (zero, zero), unroll=2)
    mq = jnp.sum(qa, axis=0, keepdims=True) * (1.0 / inner)
    mqn = jnp.sum(qn, axis=0, keepdims=True) * (1.0 / inner)

    def last(i):
        r = rows_at(i)
        dh = ((d_s[r, :] - mq - h_s[r, :] * mqn) * inv).astype(BF)
        dh2_ref[r, :] = dh
        sums_s[2, r, :] += fold(dh.astype(F32))

    loop(steps, last, 5)

    def bias(i):
        r = rows_at(i)
        bo_s[r, :] += fold(dy_ref[r, :].astype(F32))

    loop(wide // ROWS, bias, 5)
    edge_ref[...] = dh2_ref[:, 0:128].astype(F32).T[0:8, :].astype(BF)

    @pl.when(s == pl.num_programs(0) - 1)
    def _():
        for j in range(3):
            sums_ref[j : j + 1, :] = gathered_row(sums_s[j])
        bo_ref[0:1, :] = gathered_row(bo_s[...])


def conv(a1, halo, dy, mk, pc, po, vi):
    seqs, inner, length = a1.shape
    wide = dy.shape[1]
    return pl.pallas_call(
        conv_body,
        grid=(seqs,),
        in_specs=[seq((inner, length)), seq((8, inner)), seq((wide, length)), seq((8, length))]
        + [full(p.shape) for p in pc + po]
        + [full(vi.shape)],
        out_specs=[
            seq((inner, length)),
            seq((inner, length)),
            seq((8, inner)),
            full((8, inner)),
            full((8, wide)),
            full((8, length)),
            full((3, inner, inner)),
            full((wide, inner)),
        ],
        out_shape=[
            sds((seqs, inner, length), BF),
            sds((seqs, inner, length), BF),
            sds((seqs, 8, inner), BF),
            sds((8, inner), F32),
            sds((8, wide), F32),
            sds((8, length), F32),
            sds((3, inner, inner), BF),
            sds((wide, inner), BF),
        ],
        scratch_shapes=[
            pltpu.VMEM((inner, 3 * inner), BF),
            pltpu.VMEM((inner, wide), BF),
            pltpu.VMEM((3 * inner, length), BF),
            pltpu.VMEM((inner, length), F32),
            pltpu.VMEM((inner, length), F32),
            pltpu.VMEM((inner, 128), F32),
            pltpu.VMEM((3, inner, 128), F32),
            pltpu.VMEM((3, inner, 128), F32),
            pltpu.VMEM((wide, 128), F32),
            pltpu.VMEM((inner, inner), F32),
            pltpu.VMEM((inner, wide), F32),
        ],
        compiler_params=params(56),
        name="conv_and_third_norm",
    )(a1, halo, dy, mk, *pc, *po, vi)


def grad_body(a_ref, b_ref, keep_ref, send_ref, acc_s):
    s = pl.program_id(0)

    @pl.when(s == 0)
    def _():
        acc_s[...] = mm(a_ref[...], b_ref[...], NT)

    @pl.when(s > 0)
    def _():
        acc_s[...] += mm(a_ref[...], b_ref[...], NT)

    @pl.when(s == pl.num_programs(0) - 1)
    def _():
        split_grad(acc_s, keep_ref, send_ref, 0)


def grad(a, b, name):
    seqs, m, length = a.shape
    n = b.shape[1]
    size = half_of(m // 4)[1]
    return pl.pallas_call(
        grad_body,
        grid=(seqs,),
        in_specs=[seq((m, length)), seq((n, length))],
        out_specs=[full((4, size, n)), full((4, size, n))],
        out_shape=[sds((4, size, n), F32), sds((4, size, n), BF)],
        scratch_shapes=[pltpu.VMEM((m, n), F32)],
        compiler_params=params(32),
        name=name,
    )(a, b)


def shift_back(dh2_ref, halo_ref, mk_ref, hl_s, t_s):
    inner, length = dh2_ref.shape
    hl_s[...] = jnp.concatenate(
        [halo_ref[...].astype(F32), jnp.zeros((120, inner), F32)], axis=0
    ).T
    f1 = mk_ref[3:4, :]
    f2 = mk_ref[4:5, :]

    def build(i):
        r = rows_at(i)
        v = jnp.concatenate([dh2_ref[r, :].astype(F32), hl_s[r, :]], axis=1)
        t_s[0, r, :] = (pltpu.roll(v, length + 126, 1)[:, 0:length] * f1).astype(BF)
        t_s[1, r, :] = (pltpu.roll(v, length + 124, 1)[:, 0:length] * f2).astype(BF)

    loop(inner // ROWS, build, 2)


def grad_conv_body(a1_ref, dh2_ref, halo_ref, mk_ref, keep_ref, send_ref, acc_s, t_s, hl_s):
    s = pl.program_id(0)
    shift_back(dh2_ref, halo_ref, mk_ref, hl_s, t_s)

    @pl.when(s == 0)
    def _():
        acc_s[0] = mm(a1_ref[...], dh2_ref[...], NT)
        for k in (1, 2):
            acc_s[k] = mm(a1_ref[...], t_s[k - 1], NT)

    @pl.when(s > 0)
    def _():
        acc_s[0] += mm(a1_ref[...], dh2_ref[...], NT)
        for k in (1, 2):
            acc_s[k] += mm(a1_ref[...], t_s[k - 1], NT)

    @pl.when(s == pl.num_programs(0) - 1)
    def _():
        split_grad(acc_s, keep_ref, send_ref, 1)


def grad_conv(a1, dh2, halo, mk):
    seqs, inner, length = a1.shape
    size = half_of(inner // 4)[1]
    return pl.pallas_call(
        grad_conv_body,
        grid=(seqs,),
        in_specs=[
            seq((inner, length)),
            seq((inner, length)),
            seq((8, inner)),
            seq((8, length)),
        ],
        out_specs=[full((4, 3, size, inner)), full((4, 3, size, inner))],
        out_shape=[sds((4, 3, size, inner), F32), sds((4, 3, size, inner), BF)],
        scratch_shapes=[
            pltpu.VMEM((3, inner, inner), F32),
            pltpu.VMEM((2, inner, length), BF),
            pltpu.VMEM((inner, 128), F32),
        ],
        compiler_params=params(40),
        name="grad_weight_conv",
    )(a1, dh2, halo, mk)


def conv_back_body(
    dh2_ref, halo_ref, h1_ref, mk_ref, wc_ref, vi_ref,
    dh1_ref, sums_ref,
    t_s, d_s, n_s, hl_s, vi_s, sums_s,
):
    s = pl.program_id(0)
    inner, length = dh2_ref.shape
    steps = inner // ROWS

    @pl.when(s == 0)
    def _():
        sums_s[...] = jnp.zeros_like(sums_s)
        for j in range(2):
            spread(vi_ref, vi_s, j, j + 1)

    shift_back(dh2_ref, halo_ref, mk_ref, hl_s, t_s)
    d_s[...] = mm(wc_ref[0], dh2_ref[...]) + mm(wc_ref[1], t_s[0]) + mm(wc_ref[2], t_s[1])
    mean, var = row_stats(steps, lambda i: h1_ref[rows_at(i), :], inner, length)
    inv = lax.rsqrt(var + EPS)

    def back(i, acc):
        r = rows_at(i)
        n = (h1_ref[r, :] - mean) * inv
        g = col(vi_s, 0, r, length)
        z = n * g + col(vi_s, 1, r, length)
        sg = sig(z)
        e = d_s[r, :] * (sg + z * sg * (1.0 - sg))
        q = e * g
        d_s[r, :] = q
        n_s[r, :] = n
        sums_s[0, r, :] += fold(e * n)
        sums_s[1, r, :] += fold(e)
        return acc[0] + eight(q), acc[1] + eight(q * n)

    zero = jnp.zeros((8, length), F32)
    qa, qn = lax.fori_loop(0, steps, back, (zero, zero), unroll=2)
    mq = jnp.sum(qa, axis=0, keepdims=True) * (1.0 / inner)
    mqn = jnp.sum(qn, axis=0, keepdims=True) * (1.0 / inner)

    def last(i):
        r = rows_at(i)
        dh = ((d_s[r, :] - mq - n_s[r, :] * mqn) * inv).astype(BF)
        dh1_ref[r, :] = dh
        sums_s[2, r, :] += fold(dh.astype(F32))

    loop(steps, last, 5)

    @pl.when(s == pl.num_programs(0) - 1)
    def _():
        for j in range(3):
            sums_ref[j : j + 1, :] = gathered_row(sums_s[j])


def conv_back(dh2, halo, h1, mk, wc, vi):
    seqs, inner, length = dh2.shape
    return pl.pallas_call(
        conv_back_body,
        grid=(seqs,),
        in_specs=[
            seq((inner, length)),
            seq((8, inner)),
            seq((inner, length)),
            seq((8, length)),
            full(wc.shape),
            full(vi.shape),
        ],
        out_specs=[seq((inner, length)), full((8, inner))],
        out_shape=[sds((seqs, inner, length), BF), sds((8, inner), F32)],
        scratch_shapes=[
            pltpu.VMEM((2, inner, length), BF),
            pltpu.VMEM((inner, length), F32),
            pltpu.VMEM((inner, length), F32),
            pltpu.VMEM((inner, 128), F32),
            pltpu.VMEM((2, inner, 128), F32),
            pltpu.VMEM((3, inner, 128), F32),
        ],
        compiler_params=params(32),
        name="conv_backward",
    )(dh2, halo, h1, mk, wc, vi)


def stream_body(
    x_ref, dy_ref, dh1_ref, p0, p1, p2, p3, p4, vw_ref,
    gs_ref, sums_ref,
    w_s, d_s, n_s, vw_s, sums_s, sems,
):
    s = pl.program_id(0)
    wide, length = x_ref.shape
    steps = wide // ROWS

    @pl.when(s == 0)
    def _():
        copies = start_load((p0, p1, p2, p3, p4), w_s, sems)
        sums_s[...] = jnp.zeros_like(sums_s)
        for j in range(2):
            spread(vw_ref, vw_s, j, j)
        finish_load(copies)

    d_s[...] = mm(w_s[...], dh1_ref[...])
    mean, var = row_stats(steps, lambda i: x_ref[rows_at(i), :].astype(F32), wide, length)
    inv = lax.rsqrt(var + EPS)

    def back(i, acc):
        r = rows_at(i)
        n = (x_ref[r, :].astype(F32) - mean) * inv
        g = col(vw_s, 0, r, length)
        z = n * g + col(vw_s, 1, r, length)
        sg = sig(z)
        e = d_s[r, :] * (sg + z * sg * (1.0 - sg))
        q = e * g
        d_s[r, :] = q
        n_s[r, :] = n
        sums_s[0, r, :] += fold(e * n)
        sums_s[1, r, :] += fold(e)
        return acc[0] + eight(q), acc[1] + eight(q * n)

    zero = jnp.zeros((8, length), F32)
    qa, qn = lax.fori_loop(0, steps, back, (zero, zero), unroll=2)
    mq = jnp.sum(qa, axis=0, keepdims=True) * (1.0 / wide)
    mqn = jnp.sum(qn, axis=0, keepdims=True) * (1.0 / wide)

    def last(i):
        r = rows_at(i)
        gs = dy_ref[r, :].astype(F32) + (d_s[r, :] - mq - n_s[r, :] * mqn) * inv
        gs_ref[r, :] = gs.astype(BF)

    loop(steps, last, 5)

    @pl.when(s == pl.num_programs(0) - 1)
    def _():
        for j in range(2):
            sums_ref[j : j + 1, :] = gathered_row(sums_s[j])


def stream_back(x, dy, dh1, pieces, vw):
    seqs, wide, length = x.shape
    inner = dh1.shape[1]
    return pl.pallas_call(
        stream_body,
        grid=(seqs,),
        in_specs=[seq((wide, length)), seq((wide, length)), seq((inner, length))]
        + [ANY] * 5
        + [full(vw.shape)],
        out_specs=[seq((wide, length)), full((8, wide))],
        out_shape=[sds((seqs, wide, length), BF), sds((8, wide), F32)],
        scratch_shapes=[
            pltpu.VMEM((wide, inner), BF),
            pltpu.VMEM((wide, length), F32),
            pltpu.VMEM((wide, length), F32),
            pltpu.VMEM((2, wide, 128), F32),
            pltpu.VMEM((2, wide, 128), F32),
            pltpu.SemaphoreType.DMA((7,)),
        ],
        compiler_params=params(40),
        name="grad_stream",
    )(x, dy, dh1, *pieces, vw)


def output_body(x_ref, a2_ref, wt_ref, vw_ref, out_ref, sq_ref, o_s, vw_s):
    s = pl.program_id(0)
    wide, length = x_ref.shape

    @pl.when(s == 0)
    def _():
        sq_ref[...] = jnp.zeros_like(sq_ref)
        spread(vw_ref, vw_s, 0, 2)

    o_s[...] = mm(wt_ref[...], a2_ref[...])

    def close(i, acc):
        r = rows_at(i)
        branch = o_s[r, :] + col(vw_s, 0, r, length)
        result = x_ref[r, :].astype(F32) + branch
        out_ref[r, :] = result.astype(BF)
        return acc[0] + eight(branch * branch), acc[1] + eight(result * result)

    zero = jnp.zeros((8, length), F32)
    b2, r2 = lax.fori_loop(0, wide // ROWS, close, (zero, zero), unroll=5)
    sq_ref[0:1, :] += jnp.sum(b2, axis=0, keepdims=True)
    sq_ref[1:2, :] += jnp.sum(r2, axis=0, keepdims=True)


def output_of(x, a2, wt, vw):
    seqs, wide, length = x.shape
    inner = a2.shape[1]
    return pl.pallas_call(
        output_body,
        grid=(seqs,),
        in_specs=[seq((wide, length)), seq((inner, length)), full(wt.shape), full(vw.shape)],
        out_specs=[seq((wide, length)), full((8, length))],
        out_shape=[sds((seqs, wide, length), BF), sds((8, length), F32)],
        scratch_shapes=[
            pltpu.VMEM((wide, length), F32),
            pltpu.VMEM((1, wide, 128), F32),
        ],
        compiler_params=params(32),
        name="block_output",
    )(x, a2, wt, vw)


def local(
    stream, segments, cotangent, gain_zero, shift_zero, weight_in, bias_in, gain_one, shift_one,
    weight_conv, bias_conv, gain_two, shift_two, weight_out, bias_out,
):
    n_dp, n_ctx = lax.axis_size("dp"), lax.axis_size("ctx")
    assert n_dp == 4 and n_ctx & (n_ctx - 1) == 0
    me, place = lax.axis_index("dp"), lax.axis_index("ctx")
    core = place % 2
    seqs, length, wide = stream.shape
    inner = weight_conv.shape[2]
    part_w, part_i = gain_zero.shape[0], bias_in.shape[0]

    small = jnp.concatenate(
        [gain_zero, shift_zero, bias_out, bias_in, gain_one, shift_one, bias_conv, gain_two, shift_two]
    )
    piece_in = gather_pieces(weight_in, 0, core)
    near = swap(small, "dp", 1)
    pair = jnp.where(me % 2 == 0, jnp.stack([small, near]), jnp.stack([near, small]))
    far = swap(pair, "dp", 2)
    vectors = jnp.where(me < 2, jnp.concatenate([pair, far]), jnp.concatenate([far, pair]))
    vectors = vectors.astype(F32)
    vw = jnp.stack([vectors[:, j * part_w : (j + 1) * part_w].reshape(wide) for j in range(3)])
    base = 3 * part_w
    vi = jnp.stack(
        [vectors[:, base + j * part_i : base + (j + 1) * part_i].reshape(inner) for j in range(6)]
    )
    piece_conv = gather_pieces(weight_conv, 1, core)
    piece_out = gather_pieces(weight_out, 0, core)

    padded = jnp.pad(segments, ((0, 0), (4, 4)), constant_values=-1)
    near_segs = lax.dynamic_slice_in_dim(padded, place * length, length + 8, 1)
    own = near_segs[:, 4 : 4 + length]
    same = [(near_segs[:, 4 + j : 4 + j + length] == own).astype(F32) for j in (0, -2, -4, 2, 4)]
    masks = jnp.stack(same + same[:3], axis=1)

    x = jnp.swapaxes(stream, 1, 2)
    dy = jnp.swapaxes(cotangent, 1, 2)

    act_zero, hidden_one, act_one, edge, sq_one = first(x, piece_in, vw, vi)
    halo = shifted(edge, 1)
    act_two, d_hidden_two, edge_back, sums_two, sum_bo, sq_two, full_conv, full_out_t = conv(
        act_one, halo, dy, masks, piece_conv, piece_out, vi
    )
    halo_back = shifted(edge_back, -1)
    keep_out, send_out = grad(act_two, dy, "grad_weight_out")
    keep_conv, send_conv = grad_conv(act_one, d_hidden_two, halo_back, masks)
    d_hidden_one, sums_one = conv_back(d_hidden_two, halo_back, hidden_one, masks, full_conv, vi)
    keep_in, send_in = grad(act_zero, d_hidden_one, "grad_weight_in")
    grad_x, sums_zero = stream_back(x, dy, d_hidden_one, piece_in, vw)
    output, sq_out = output_of(x, act_two, full_out_t, vw)

    sum_out = sum_shards(keep_out, send_out)
    sum_conv = sum_shards(keep_conv, send_conv)
    sum_in = sum_shards(keep_in, send_in)
    grad_weight_out = join_halves(*sum_out, part_i, 0, core)
    grad_weight_conv = join_halves(*sum_conv, part_i, 1, core)
    grad_weight_in = join_halves(*sum_in, part_w, 0, core)

    def padded_scalars(values):
        return jnp.pad(jnp.stack(values), (0, 128 - len(values)))

    early = sum_all(
        jnp.concatenate(
            [
                sum_bo[0],
                sums_one[0:3].reshape(-1),
                sums_two[0:3].reshape(-1),
                padded_scalars([jnp.sum(sq_one[0]), jnp.sum(sq_one[1]), jnp.sum(sq_two[0])]),
            ]
        )
    )
    late = sum_all(
        jnp.concatenate(
            [
                sums_zero[0:2].reshape(-1),
                padded_scalars([jnp.sum(sq_out[0]), jnp.sum(sq_out[1])]),
            ]
        )
    )

    def part(values, begin, size):
        return lax.dynamic_slice_in_dim(values, begin + me * size, size)

    at = wide
    grad_gain_one = part(early, at, part_i)
    grad_shift_one = part(early, at + inner, part_i)
    grad_bias_in = part(early, at + 2 * inner, part_i)
    grad_gain_two = part(early, at + 3 * inner, part_i)
    grad_shift_two = part(early, at + 4 * inner, part_i)
    grad_bias_conv = part(early, at + 5 * inner, part_i)
    grad_bias_out = part(early, 0, part_w)
    grad_gain_zero = part(late, 0, part_w)
    grad_shift_zero = part(late, wide, part_w)
    count = float(seqs * length * n_dp * n_ctx)
    sq_at = at + 6 * inner
    rms_in = jnp.sqrt(early[sq_at] / (count * wide))
    rms_hidden_one = jnp.sqrt(early[sq_at + 1] / (count * inner))
    rms_hidden_two = jnp.sqrt(early[sq_at + 2] / (count * inner))
    rms_branch = jnp.sqrt(late[2 * wide] / (count * wide))
    rms_out = jnp.sqrt(late[2 * wide + 1] / (count * wide))
    return (
        jnp.swapaxes(output, 1, 2),
        jnp.swapaxes(grad_x, 1, 2),
        grad_gain_zero,
        grad_shift_zero,
        grad_weight_in,
        grad_bias_in,
        grad_gain_one,
        grad_shift_one,
        grad_weight_conv,
        grad_bias_conv,
        grad_gain_two,
        grad_shift_two,
        grad_weight_out,
        grad_bias_out,
        rms_in,
        rms_out,
        rms_hidden_one,
        rms_hidden_two,
        rms_branch,
    )


def solution(mesh):
    placed = (
        P("dp", "ctx", None),
        P("dp", None),
        P("dp", "ctx", None),
        P("dp"),
        P("dp"),
        P("dp", None),
        P("dp"),
        P("dp"),
        P("dp"),
        P(None, "dp", None),
        P("dp"),
        P("dp"),
        P("dp"),
        P("dp", None),
        P("dp"),
    )
    return jax.shard_map(
        local,
        mesh=mesh,
        in_specs=placed,
        out_specs=(
            P("dp", "ctx", None),
            P("dp", "ctx", None),
            P("dp"),
            P("dp"),
            P("dp", None),
            P("dp"),
            P("dp"),
            P("dp"),
            P(None, "dp", None),
            P("dp"),
            P("dp"),
            P("dp"),
            P("dp", None),
            P("dp"),
            P(),
            P(),
            P(),
            P(),
            P(),
        ),
        check_vma=False,
    )
```

time: 581 us -> 423 us (0.73)
  Pallas kernels: 0 us -> 190 us
  matrix products: 129 us -> 0 us
  blocking collectives: 103 us -> 0 us
  other arithmetic: 118 us -> 23.9 us
  starting transfers between devices: 2.86 us -> 55.2 us
  local copies, waits for them, and re-layouts: 86 us -> 44 us
  between operations: 26.9 us -> 10.7 us
  waiting for transfers between devices: 109 us -> 99.2 us
    pallas_call x0 -> x8, Pallas kernels: none -> 190 us  [the longest x1 47.8 us: conv(): pl.pallas_call(conv_body, grid=(seqs,), in_specs=[seq((inner, length)), s...]
    dot_general x9 -> x0, matrix products: 129 us -> none  [the longest x1 23 us: local(): jnp.dot(act_two, full_wout, preferred_element_type=jnp.float32)]
    ppermute x2 -> x44, waiting for transfers between devices: 0.01 us -> 99.2 us  [the longest x30 62 us: swap(): lax.ppermute(value, axis, [(i, i ^ mask) for i in range(lax.axis_size(axi...]
    psum x2 -> x0, blocking collectives: 68.3 us -> none  [the longest x1 41.2 us: local(): totals = lax.psum(local_squares, ('dp', 'ctx'))]
    ppermute x2 -> x44, starting transfers between devices: 2.59 us -> 55.2 us  [the longest x30 32.1 us: swap(): lax.ppermute(value, axis, [(i, i ^ mask) for i in range(lax.axis_size(axi...]
    psum x1 -> x0, waiting for transfers between devices: 48 us -> none  [local(): lax.psum((grad_terms[0], grad_terms[1], grad_terms[2], grad_terms[3], gra...]
    reduce_scatter x1 -> x0, waiting for transfers between devices: 46.5 us -> none  [local(): lax.psum_scatter(whole_sums[6], 'dp', scatter_dimension=1, tiled=True)]
    unnamed x2 -> x0, blocking collectives: 34.8 us -> none
  transfers between devices with their start and end apart: 9 -> 44, of which waited for: 3 -> 19; matrix products, arithmetic and copies ran while one was open for 50% -> 9% of each run, Pallas kernels for 0% -> 32%
where the time goes in v1:
time: 423 us; the launch traced here: 422 us
  Pallas kernels  190 us (45%)
  waiting for transfers between devices  99.2 us (23%)
  starting transfers between devices  55.2 us (13%)
  local copies, waits for them, and re-layouts  44 us (10%)
  other arithmetic  23.9 us (6%)
  between operations  10.7 us (3%)
    ppermute x30, waiting for transfers between devices, swap(): lax.ppermute(value, axis, [(i, i ^ mask) for i in range(lax.axis_size(axi...  62 us
    pallas_call x1, Pallas kernels, conv(): pl.pallas_call(conv_body, grid=(seqs,), in_specs=[seq((inner, length)), s...  47.8 us
    ppermute x12, waiting for transfers between devices, by_core(): return lax.ppermute(value, ('dp', 'ctx'), pairs)  37.1 us
    ppermute x30, starting transfers between devices, swap(): lax.ppermute(value, axis, [(i, i ^ mask) for i in range(lax.axis_size(axi...  32.1 us
    pallas_call x1, Pallas kernels, stream_back(): pl.pallas_call(stream_body, grid=(seqs,), in_specs=[seq((wide, length)),...  31 us
    pallas_call x1, Pallas kernels, conv_back(): pl.pallas_call(conv_back_body, grid=(seqs,), in_specs=[seq((inner, length...  30.6 us
    unnamed x90, local copies, waits for them, and re-layouts  28.6 us
    pallas_call x1, Pallas kernels, first(): pl.pallas_call(first_body, grid=(seqs,), in_specs=[seq((wide, length))] +...  26.5 us
  transfers between devices with their start and end apart: 44, of which 19 were waited for; matrix products, arithmetic and copies ran while one was open for 9% of the time, Pallas kernels for 32%

profile of v1, /device:TPU:0, one launch (start us, length us, event | category | flops | bytes accessed | tf_op | source)
XLA Modules:
  0.0 422.5 jit_solution(15916978089403189119)
XLA Ops:
  1.9 3.0 collective-permute-start.7
  4.9 6.2 %concatenate.24 = bf16[2400]{0:T(1024)(128)(2,1)S(1)} concatenate(bf16[400]{0:T(512)(128)(2,1)} %param.18, bf16[400]{0:T(512)(128)(2,1)} %param.19, bf16[400]{0:T(512)(128)(2,1)} %param.29, bf16[200]{0:T(256)(128)(2,1)} %param.21, bf16[200]{0:T(256)(128)(2,1)} %param.22, bf16[200]{0:T(256)(128)(2,1)} %param.23, bf16[200]{0:T(256)(128)(2,1)} %param.25, bf16[200]{0:T(256)(128)(2,1)} %param.26, ...), dimensions={0} | concatenate | bytes 9600 | tf_op jit(solution)/shard_map/concatenate | solution.py:765
  18.6 4.1 collective-permute-done.11.o1
  24.6 2.6 collective-permute-start.12
  27.2 3.4 collective-permute-done.p1
  31.6 2.6 collective-permute-start.1
  36.6 15.2 %collective-permute-done.5 = bf16[2,2400]{1,0:T(2,128)(2,1)S(1)} collective-permute-done((bf16[2,2400]{1,0:T(2,128)(2,1)S(1)}, bf16[2,2400]{1,0:T(2,128)(2,1)S(1)}, u32[]{:S(2)}, u32[]{:S(2)}) %collective-permute-start.5) | collective-permute-done | bytes 9632 | tf_op jit(solution)/shard_map/ppermute | solution.py:27
  56.3 26.5 %norm_and_first_product.1 = (bf16[4,1600,512]{2,1,0:T(8,128)(2,1)S(1)}, f32[4,800,512]{2,1,0:T(8,128)}, bf16[4,800,512]{2,1,0:T(8,128)(2,1)S(1)}, bf16[4,8,800]{2,1,0:T(8,128)(2,1)S(1)}, f32[8,512]{1,0:T(8,128)S(1)}) custom-call(bf16[4,1600,512]{2,1,0:T(8,128)(2,1)} %bitcast.53, bf16[400,800]{1,0:T(8,128)(2,1)S(1)} %copy-done.10, ...), custom_call_target="tpu_custom_call" | custom-call | tf_op jit(solution)/shard_map/norm_and_first_product/pallas_call | solution.py:293
  84.5 2.7 copy-done.12
  91.3 47.8 %conv_and_third_norm.1 = (bf16[4,800,512]{2,1,0:T(8,128)(2,1)}, bf16[4,800,512]{2,1,0:T(8,128)(2,1)}, bf16[4,8,800]{2,1,0:T(8,128)(2,1)}, f32[8,800]{1,0:T(8,128...) custom-call(bf16[4,800,512]{2,1,0:T(8,128)(2,1)} %copy-done.2, ...), custom_call_target="tpu_custom_call" | custom-call | tf_op jit(solution)/shard_map/conv_and_third_norm/pallas_call | solution.py:415
  139.2 2.9 copy-done.1
  143.9 8.2 %grad_weight_out.1 = (f32[4,104,1600]{2,1,0:T(8,128)S(1)}, bf16[4,104,1600]{2,1,0:T(8,128)(2,1)}) custom-call(bf16[4,800,512]{2,1,0:T(8,128)(2,1)S(1)} %copy-done.6, bf16[4,1600,512]{2,1,0:T(8,128)(2,1)S(1)} %bitcast.60), custom_call_target="tpu_custom_call" | custom-call | tf_op jit(solution)/shard_map/grad_weight_out/pallas_call | solution.py:479
  155.7 12.8 %block_output.1 = (bf16[4,1600,512]{2,1,0:T(8,128)(2,1)}, f32[8,512]{1,0:T(8,128)S(1)}) custom-call(bf16[4,1600,512]{2,1,0:T(8,128)(2,1)S(1)} %bitcast.56, bf16[4,800,512]{2,1,0:T(8,128)(2,1)S(1)} %copy-done.7, bf16[1600,800]{1,0:T(8,128)(2,1)S(1)} %copy-done.25, f32[3,1600]{1,0:T(4,128)S(1)} %pad_maximum_fusion.6.vw_ref), custom_call_target="tpu_custom_call" | custom-call | tf_op jit(solution)/shard_map/block_output/pallas_call | solution.py:738
  171.9 2.9 copy-done.14
  177.0 30.6 %conv_backward.1 = (bf16[4,800,512]{2,1,0:T(8,128)(2,1)S(1)}, f32[8,800]{1,0:T(8,128)S(1)}) custom-call(bf16[4,800,512]{2,1,0:T(8,128)(2,1)S(1)} %copy-done.4, bf16[4,8,800]{2,1,0:T(8,128)(2,1)S(1)} %collective-permute-done.15.halo_ref, f32[4,800,512]{2,1,0:T(8,128)S(1)} %copy-done.14, f32[4,8,512]{2,1,0:T(8,128)S(1)} %copy-done.30, ...), custom_call_target="tpu_custom_call" | custom-call | tf_op jit(solution)/shard_map/conv_backward/pallas_call | solution.py:608
  207.6 4.0 copy-done.13
  211.6 9.1 %grad_weight_in.1 = (f32[4,208,800]{2,1,0:T(8,128)S(1)}, bf16[4,208,800]{2,1,0:T(8,128)(2,1)}) custom-call(bf16[4,1600,512]{2,1,0:T(8,128)(2,1)S(1)} %copy-done.13, bf16[4,800,512]{2,1,0:T(8,128)(2,1)S(1)} %get-tuple-element.53.dh1_ref.b_ref), custom_call_target="tpu_custom_call" | custom-call | tf_op jit(solution)/shard_map/grad_weight_in/pallas_call | solution.py:479
  228.7 23.5 %grad_weight_conv.1 = (f32[4,3,104,800]{3,2,1,0:T(8,128)S(1)}, bf16[4,3,104,800]{3,2,1,0:T(8,128)(2,1)}) custom-call(bf16[4,800,512]{2,1,0:T(8,128)(2,1)S(1)} %copy-done.3, bf16[4,800,512]{2,1,0:T(8,128)(2,1)S(1)} %copy-done.5, bf16[4,8,800]{2,1,0:T(8,128)(2,1)S(1)} %collective-permute-done.15.halo_ref, f32[4,8,512]{2,1,0:T(8,128)S(1)} %copy-done.30), custom_call_target="tpu_custom_call" | custom-call | tf_op jit(solution)/shard_map/grad_weight_conv/pallas_call | solution.py:532
  254.9 2.9 copy-done
  257.7 31.0 %grad_stream.1 = (bf16[4,1600,512]{2,1,0:T(8,128)(2,1)}, f32[8,1600]{1,0:T(8,128)S(1)}) custom-call(bf16[4,1600,512]{2,1,0:T(8,128)(2,1)S(1)} %bitcast.57, bf16[4,1600,512]{2,1,0:T(8,128)(2,1)} %bitcast.59, bf16[4,800,512]{2,1,0:T(8,128)(2,1)S(1)} %copy-done.9, bf16[400,800]{1,0:T(8,128)(2,1)S(1)} %copy-done.11, bf16[208,800]{1,0:T(8,128)(2,1)S(1)} %copy-done.18, ...), custom_call_target="tpu_custom_call" | custom-call | tf_op jit(solution)/shard_map/grad_stream/pallas_call | solution.py:690
  295.6 8.7 %collective-permute-done.17 = f32[3328]{0:T(1024)S(1)} collective-permute-done((f32[3328]{0:T(1024)S(1)}, f32[3328]{0:T(1024)S(1)}, u32[]{:S(2)}, u32[]{:S(2)}) %collective-permute-start.17) | collective-permute-done | bytes 13344 | tf_op jit(solution)/shard_map/ppermute | solution.py:27
  305.2 2.7 collective-permute-done.18
  312.0 3.1 collective-permute-start.20
  321.0 2.9 collective-permute-start.31
  334.2 9.8 %collective-permute-done.22 = bf16[2,208,800]{2,1,0:T(8,128)(2,1)S(1)} collective-permute-done((bf16[2,208,800]{2,1,0:T(8,128)(2,1)S(1)}, bf16[2,208,800]{2,1,0:T(8,128)(2,1)S(1)}, u32[]{:S(2)}, u32[]{:S(2)}) %collective-permute-start.22) | collective-permute-done | bytes 665632 | tf_op jit(solution)/shard_map/ppermute | solution.py:23
  347.3 4.5 %collective-permute-done.23 = bf16[208,800]{1,0:T(8,128)(2,1)S(1)} collective-permute-done((bf16[208,800]{1,0:T(8,128)(2,1)S(1)}, bf16[208,800]{1,0:T(8,128)(2,1)S(1)}, u32[]{:S(2)}, u32[]{:S(2)}) %collective-permute-start.23) | collective-permute-done | bytes 332832 | tf_op jit(solution)/shard_map/ppermute | solution.py:23
  353.8 8.1 %collective-permute-done.33 = bf16[2,3,104,800]{3,2,1,0:T(8,128)(2,1)S(1)} collective-permute-done((bf16[2,3,104,800]{3,2,1,0:T(8,128)(2,1)S(1)}, bf16[2,3,104,800]{3,2,1,0:T(8,128)(2,1)S(1)}, u32[]{:S(2)}, u32[]{:S(2)}) %collective-permute-start.33) | collective-permute-done | bytes 998432 | tf_op jit(solution)/shard_map/ppermute | solution.py:23
  363.6 2.8 collective-permute-start.42
  366.8 5.1 %collective-permute-done.34 = bf16[3,104,800]{2,1,0:T(8,128)(2,1)S(1)} collective-permute-done((bf16[3,104,800]{2,1,0:T(8,128)(2,1)S(1)}, bf16[3,104,800]{2,1,0:T(8,128)(2,1)S(1)}, u32[]{:S(2)}, u32[]{:S(2)}) %collective-permute-start.34) | collective-permute-done | bytes 499232 | tf_op jit(solution)/shard_map/ppermute | solution.py:23
  378.7 5.0 %collective-permute-done.25 = bf16[208,800]{1,0:T(8,128)(2,1)S(1)} collective-permute-done((bf16[208,800]{1,0:T(8,128)(2,1)S(1)}, bf16[208,800]{1,0:T(8,128)(2,1)S(1)}, u32[]{:S(2)}, u32[]{:S(2)}) %collective-permute-start.25) | collective-permute-done | bytes 332832 | tf_op jit(solution)/shard_map/ppermute | solution.py:27
  385.2 4.1 collective-permute-start.36
  389.5 22.5 %collective-permute-done.36 = bf16[3,104,800]{2,1,0:T(8,128)(2,1)S(1)} collective-permute-done((bf16[3,104,800]{2,1,0:T(8,128)(2,1)S(1)}, bf16[3,104,800]{2,1,0:T(8,128)(2,1)S(1)}, u32[]{:S(2)}, u32[]{:S(2)}) %collective-permute-start.36) | collective-permute-done | bytes 499232 | tf_op jit(solution)/shard_map/ppermute | solution.py:27
  (249 shorter events, 90.6 us)
Async XLA Ops:
  1.9 13.2 %collective-permute-start.7 = (bf16[3,104,800]{2,1,0:T(8,128)(2,1)S(1)}, bf16[3,104,800]{2,1,0:T(8,128)(2,1)}, u32[]{:S(2)}, u32[]{:S(2)}) collective-permute-start(bf16[3,104,800]{2,1,0:T(8,128)(2,1)S(1)} %constant_dynamic-slice_fusion.1), channel_id=1, source_target_pairs={{0,8},{1,17},{2,10},{3,19},{4,12},{5,21},{6,14},{7,23},{8,0},{9,25... | collective-permute-start | bytes 1497608 | tf_op jit(solution)/shard_map/ppermute | solution.py:23
  12.9 9.8 %collective-permute-start.11 = (bf16[104,1600]{1,0:T(8,128)(2,1)}, bf16[104,1600]{1,0:T(8,128)(2,1)}, u32[]{:S(2)}, u32[]{:S(2)}) collective-permute-start(bf16[104,1600]{1,0:T(8,128)(2,1)} %constant_dynamic-slice_fusion), channel_id=1, source_target_pairs={{0,8},{1,17},{2,10},{3,19},{4,12},{5,21},{6,14},{7,23},{8,0},{9,25... | collective-permute-start | bytes 998408 | tf_op jit(solution)/shard_map/ppermute | solution.py:23
  15.0 15.6 %collective-permute-start = (bf16[208,800]{1,0:T(8,128)(2,1)S(1)}, bf16[208,800]{1,0:T(8,128)(2,1)S(1)}, u32[]{:S(2)}, u32[]{:S(2)}) collective-permute-start(bf16[208,800]{1,0:T(8,128)(2,1)S(1)} %constant_dynamic-slice_fusion.2), channel_id=1, source_target_pairs={{0,8},{1,17},{2,10},{3,19},{4,12},{5,21},{6,14},{7,23},{8,0},{9,25... | collective-permute-start | bytes 998408 | tf_op jit(solution)/shard_map/ppermute | solution.py:23
  16.4 20.0 %collective-permute-start.8 = (bf16[2,3,104,800]{3,2,1,0:T(8,128)(2,1)S(1)}, bf16[2,3,104,800]{3,2,1,0:T(8,128)(2,1)}, u32[]{:S(2)}, u32[]{:S(2)}) collective-permute-start(bf16[2,3,104,800]{3,2,1,0:T(8,128)(2,1)S(1)} %pad_maximum_fusion.3), channel_id=1, source_target_pairs={{0,16},{1,9},{2,18},{3,11},{4,20},{5,13},{6,22},{7,15},{8,24},{9,1... | collective-permute-start | bytes 2995208 | tf_op jit(solution)/shard_map/ppermute | solution.py:23
  24.6 27.3 %collective-permute-start.12 = (bf16[2,104,1600]{2,1,0:T(8,128)(2,1)}, bf16[2,104,1600]{2,1,0:T(8,128)(2,1)}, u32[]{:S(2)}, u32[]{:S(2)}) collective-permute-start(bf16[2,104,1600]{2,1,0:T(8,128)(2,1)} %pad_maximum_fusion.5), channel_id=1, source_target_pairs={{0,16},{1,9},{2,18},{3,11},{4,20},{5,13},{6,22},{7,15},{8,24},{9,1... | collective-permute-start | bytes 1996808 | tf_op jit(solution)/shard_map/ppermute | solution.py:23
  31.6 20.9 %collective-permute-start.1 = (bf16[2,208,800]{2,1,0:T(8,128)(2,1)}, bf16[2,208,800]{2,1,0:T(8,128)(2,1)S(1)}, u32[]{:S(2)}, u32[]{:S(2)}) collective-permute-start(bf16[2,208,800]{2,1,0:T(8,128)(2,1)} %pad_maximum_fusion.4), channel_id=1, source_target_pairs={{0,16},{1,9},{2,18},{3,11},{4,20},{5,13},{6,22},{7,15},{8,24},{9,1... | collective-permute-start | bytes 1996808 | tf_op jit(solution)/shard_map/ppermute | solution.py:23
  34.2 17.6 %collective-permute-start.5 = (bf16[2,2400]{1,0:T(2,128)(2,1)S(1)}, bf16[2,2400]{1,0:T(2,128)(2,1)S(1)}, u32[]{:S(2)}, u32[]{:S(2)}) collective-permute-start(bf16[2,2400]{1,0:T(2,128)(2,1)S(1)} %broadcast_select_fusion.3), channel_id=1, source_target_pairs={{0,16},{8,24},{16,0},{24,8},{1,17},{9,25},{17,1},{25,9},{2,18},{10... | collective-permute-start | bytes 28808 | tf_op jit(solution)/shard_map/ppermute | solution.py:27
  36.4 54.3 %collective-permute-start.10 = (bf16[2,3,104,800]{3,2,1,0:T(8,128)(2,1)}, bf16[2,3,104,800]{3,2,1,0:T(8,128)(2,1)}, u32[]{:S(2)}, u32[]{:S(2)}) collective-permute-start(bf16[2,3,104,800]{3,2,1,0:T(8,128)(2,1)} %collective-permute-done.8.c2), channel_id=1, source_target_pairs={{0,1},{1,0},{2,3},{3,2},{4,5},{5,4},{6,7},{7,6},{8,9},{9,8},{10,11... | collective-permute-start | bytes 2995208 | tf_op jit(solution)/shard_map/ppermute | solution.py:27
  51.9 38.7 %collective-permute-start.14 = (bf16[2,104,1600]{2,1,0:T(8,128)(2,1)}, bf16[2,104,1600]{2,1,0:T(8,128)(2,1)}, u32[]{:S(2)}, u32[]{:S(2)}) collective-permute-start(bf16[2,104,1600]{2,1,0:T(8,128)(2,1)} %collective-permute-done.12.o2), channel_id=1, source_target_pairs={{0,1},{1,0},{2,3},{3,2},{4,5},{5,4},{6,7},{7,6},{8,9},{9,8},{10,11... | collective-permute-start | bytes 1996808 | tf_op jit(solution)/shard_map/ppermute | solution.py:27
  52.7 38.0 %collective-permute-start.9 = (bf16[3,104,800]{2,1,0:T(8,128)(2,1)}, bf16[3,104,800]{2,1,0:T(8,128)(2,1)}, u32[]{:S(2)}, u32[]{:S(2)}) collective-permute-start(bf16[3,104,800]{2,1,0:T(8,128)(2,1)} %collective-permute-done.7.c1), channel_id=1, source_target_pairs={{0,1},{1,0},{2,3},{3,2},{4,5},{5,4},{6,7},{7,6},{8,9},{9,8},{10,11... | collective-permute-start | bytes 1497608 | tf_op jit(solution)/shard_map/ppermute | solution.py:27
  54.0 36.6 %collective-permute-start.13 = (bf16[104,1600]{1,0:T(8,128)(2,1)}, bf16[104,1600]{1,0:T(8,128)(2,1)}, u32[]{:S(2)}, u32[]{:S(2)}) collective-permute-start(bf16[104,1600]{1,0:T(8,128)(2,1)} %collective-permute-done.11.o1), channel_id=1, source_target_pairs={{0,1},{1,0},{2,3},{3,2},{4,5},{5,4},{6,7},{7,6},{8,9},{9,8},{10,11... | collective-permute-start | bytes 998408 | tf_op jit(solution)/shard_map/ppermute | solution.py:27
  152.1 136.8 %collective-permute-start.38 = (bf16[4,104,1600]{2,1,0:T(8,128)(2,1)}, bf16[4,104,1600]{2,1,0:T(8,128)(2,1)}, u32[]{:S(2)}, u32[]{:S(2)}) collective-permute-start(bf16[4,104,1600]{2,1,0:T(8,128)(2,1)} %get-tuple-element.68), channel_id=1, source_target_pairs={{0,1},{1,0},{2,3},{3,2},{4,5},{5,4},{6,7},{7,6},{8,9},{9,8},{10,11... | collective-permute-start | bytes 3993608 | tf_op jit(solution)/shard_map/ppermute | solution.py:27
  154.1 17.7 %collective-permute-start.15 = (bf16[4,8,800]{2,1,0:T(8,128)(2,1)S(1)}, bf16[4,8,800]{2,1,0:T(8,128)(2,1)S(1)}, u32[]{:S(2)}, u32[]{:S(2)}) collective-permute-start(bf16[4,8,800]{2,1,0:T(8,128)(2,1)S(1)} %copy-done.40), channel_id=1, source_target_pairs={{1,0},{2,1},{3,2},{4,3},{5,4},{6,5},{7,6},{9,8},{10,9},{11,10},{12... | collective-permute-start | bytes 153608 | tf_op jit(solution)/shard_map/ppermute | solution.py:32
  222.4 103.6 %collective-permute-start.21 = (bf16[4,208,800]{2,1,0:T(8,128)(2,1)}, bf16[4,208,800]{2,1,0:T(8,128)(2,1)}, u32[]{:S(2)}, u32[]{:S(2)}) collective-permute-start(bf16[4,208,800]{2,1,0:T(8,128)(2,1)} %get-tuple-element.59), channel_id=1, source_target_pairs={{0,1},{1,0},{2,3},{3,2},{4,5},{5,4},{6,7},{7,6},{8,9},{9,8},{10,11... | collective-permute-start | bytes 3993608 | tf_op jit(solution)/shard_map/ppermute | solution.py:27
  226.6 67.9 %collective-permute-start.27 = (f32[6528]{0:T(1024)S(1)}, f32[6528]{0:T(1024)S(1)}, u32[]{:S(2)}, u32[]{:S(2)}) collective-permute-start(f32[6528]{0:T(1024)S(1)} %concatenate.29), channel_id=1, source_target_pairs={{0,1},{1,0},{2,3},{3,2},{4,5},{5,4},{6,7},{7,6},{8,9},{9,8},{10,11... | collective-permute-start | bytes 78344 | tf_op jit(solution)/shard_map/ppermute | solution.py:27
  254.4 76.6 %collective-permute-start.32 = (bf16[4,3,104,800]{3,2,1,0:T(8,128)(2,1)}, bf16[4,3,104,800]{3,2,1,0:T(8,128)(2,1)}, u32[]{:S(2)}, u32[]{:S(2)}) collective-permute-start(bf16[4,3,104,800]{3,2,1,0:T(8,128)(2,1)} %get-tuple-element.66), channel_id=1, source_target_pairs={{0,1},{1,0},{2,3},{3,2},{4,5},{5,4},{6,7},{7,6},{8,9},{9,8},{10,11... | collective-permute-start | bytes 5990408 | tf_op jit(solution)/shard_map/ppermute | solution.py:27
  292.4 37.3 %collective-permute-start.39 = (bf16[2,104,1600]{2,1,0:T(8,128)(2,1)}, bf16[2,104,1600]{2,1,0:T(8,128)(2,1)S(1)}, u32[]{:S(2)}, u32[]{:S(2)}) collective-permute-start(bf16[2,104,1600]{2,1,0:T(8,128)(2,1)} %fusion.2), channel_id=1, source_target_pairs={{0,8},{1,17},{2,10},{3,19},{4,12},{5,21},{6,14},{7,23},{8,0},{9,25... | collective-permute-start | bytes 1996808 | tf_op jit(solution)/shard_map/ppermute | solution.py:23
  293.4 10.8 %collective-permute-start.17 = (f32[3328]{0:T(1024)S(1)}, f32[3328]{0:T(1024)S(1)}, u32[]{:S(2)}, u32[]{:S(2)}) collective-permute-start(f32[3328]{0:T(1024)S(1)} %fusion.31), channel_id=1, source_target_pairs={{0,8},{8,0},{16,24},{24,16},{1,9},{9,1},{17,25},{25,17},{2,10},{10... | collective-permute-start | bytes 39944 | tf_op jit(solution)/shard_map/ppermute | solution.py:27
  294.5 15.8 %collective-permute-start.28 = (f32[6528]{0:T(1024)S(1)}, f32[6528]{0:T(1024)S(1)}, u32[]{:S(2)}, u32[]{:S(2)}) collective-permute-start(f32[6528]{0:T(1024)S(1)} %add.212), channel_id=1, source_target_pairs={{0,8},{8,0},{16,24},{24,16},{1,9},{9,1},{17,25},{25,17},{2,10},{10... | collective-permute-start | bytes 78344 | tf_op jit(solution)/shard_map/ppermute | solution.py:27
  328.4 15.6 %collective-permute-start.22 = (bf16[2,208,800]{2,1,0:T(8,128)(2,1)S(1)}, bf16[2,208,800]{2,1,0:T(8,128)(2,1)S(1)}, u32[]{:S(2)}, u32[]{:S(2)}) collective-permute-start(bf16[2,208,800]{2,1,0:T(8,128)(2,1)S(1)} %fusion.1), channel_id=1, source_target_pairs={{0,8},{1,17},{2,10},{3,19},{4,12},{5,21},{6,14},{7,23},{8,0},{9,25... | collective-permute-start | bytes 1996808 | tf_op jit(solution)/shard_map/ppermute | solution.py:23
  329.9 15.6 %collective-permute-start.40 = (bf16[104,1600]{1,0:T(8,128)(2,1)S(1)}, bf16[104,1600]{1,0:T(8,128)(2,1)S(1)}, u32[]{:S(2)}, u32[]{:S(2)}) collective-permute-start(bf16[104,1600]{1,0:T(8,128)(2,1)S(1)} %fusion.17), channel_id=1, source_target_pairs={{0,16},{1,9},{2,18},{3,11},{4,20},{5,13},{6,22},{7,15},{8,24},{9,1... | collective-permute-start | bytes 998408 | tf_op jit(solution)/shard_map/ppermute | solution.py:23
  333.2 28.8 %collective-permute-start.33 = (bf16[2,3,104,800]{3,2,1,0:T(8,128)(2,1)S(1)}, bf16[2,3,104,800]{3,2,1,0:T(8,128)(2,1)S(1)}, u32[]{:S(2)}, u32[]{:S(2)}) collective-permute-start(bf16[2,3,104,800]{3,2,1,0:T(8,128)(2,1)S(1)} %fusion), channel_id=1, source_target_pairs={{0,8},{1,17},{2,10},{3,19},{4,12},{5,21},{6,14},{7,23},{8,0},{9,25... | collective-permute-start | bytes 2995208 | tf_op jit(solution)/shard_map/ppermute | solution.py:23
  344.2 7.6 %collective-permute-start.23 = (bf16[208,800]{1,0:T(8,128)(2,1)S(1)}, bf16[208,800]{1,0:T(8,128)(2,1)S(1)}, u32[]{:S(2)}, u32[]{:S(2)}) collective-permute-start(bf16[208,800]{1,0:T(8,128)(2,1)S(1)} %fusion.16), channel_id=1, source_target_pairs={{0,16},{1,9},{2,18},{3,11},{4,20},{5,13},{6,22},{7,15},{8,24},{9,1... | collective-permute-start | bytes 998408 | tf_op jit(solution)/shard_map/ppermute | solution.py:23
  345.6 17.9 %collective-permute-start.41 = (bf16[104,1600]{1,0:T(8,128)(2,1)S(1)}, bf16[104,1600]{1,0:T(8,128)(2,1)S(1)}, u32[]{:S(2)}, u32[]{:S(2)}) collective-permute-start(bf16[104,1600]{1,0:T(8,128)(2,1)S(1)} %fusion.14), channel_id=1, source_target_pairs={{0,2},{1,3},{2,0},{3,1},{4,6},{5,7},{6,4},{7,5},{8,10},{9,11},{10,... | collective-permute-start | bytes 998408 | tf_op jit(solution)/shard_map/ppermute | solution.py:27
  352.0 14.4 %collective-permute-start.24 = (bf16[208,800]{1,0:T(8,128)(2,1)S(1)}, bf16[208,800]{1,0:T(8,128)(2,1)S(1)}, u32[]{:S(2)}, u32[]{:S(2)}) collective-permute-start(bf16[208,800]{1,0:T(8,128)(2,1)S(1)} %fusion.10), channel_id=1, source_target_pairs={{0,2},{1,3},{2,0},{3,1},{4,6},{5,7},{6,4},{7,5},{8,10},{9,11},{10,... | collective-permute-start | bytes 998408 | tf_op jit(solution)/shard_map/ppermute | solution.py:27
  362.3 9.6 %collective-permute-start.34 = (bf16[3,104,800]{2,1,0:T(8,128)(2,1)S(1)}, bf16[3,104,800]{2,1,0:T(8,128)(2,1)S(1)}, u32[]{:S(2)}, u32[]{:S(2)}) collective-permute-start(bf16[3,104,800]{2,1,0:T(8,128)(2,1)S(1)} %fusion.15), channel_id=1, source_target_pairs={{0,16},{1,9},{2,18},{3,11},{4,20},{5,13},{6,22},{7,15},{8,24},{9,1... | collective-permute-start | bytes 1497608 | tf_op jit(solution)/shard_map/ppermute | solution.py:23
  363.6 10.9 %collective-permute-start.42 = (bf16[104,1600]{1,0:T(8,128)(2,1)S(1)}, bf16[104,1600]{1,0:T(8,128)(2,1)S(1)}, u32[]{:S(2)}, u32[]{:S(2)}) collective-permute-start(bf16[104,1600]{1,0:T(8,128)(2,1)S(1)} %add_convert_fusion.2), channel_id=1, source_target_pairs={{0,4},{1,5},{2,6},{3,7},{4,0},{5,1},{6,2},{7,3},{8,12},{9,13},{10,... | collective-permute-start | bytes 998408 | tf_op jit(solution)/shard_map/ppermute | solution.py:27
  366.5 17.2 %collective-permute-start.25 = (bf16[208,800]{1,0:T(8,128)(2,1)S(1)}, bf16[208,800]{1,0:T(8,128)(2,1)S(1)}, u32[]{:S(2)}, u32[]{:S(2)}) collective-permute-start(bf16[208,800]{1,0:T(8,128)(2,1)S(1)} %add_convert_fusion.1), channel_id=1, source_target_pairs={{0,4},{1,5},{2,6},{3,7},{4,0},{5,1},{6,2},{7,3},{8,12},{9,13},{10,... | collective-permute-start | bytes 998408 | tf_op jit(solution)/shard_map/ppermute | solution.py:27
  372.1 13.0 %collective-permute-start.35 = (bf16[3,104,800]{2,1,0:T(8,128)(2,1)S(1)}, bf16[3,104,800]{2,1,0:T(8,128)(2,1)S(1)}, u32[]{:S(2)}, u32[]{:S(2)}) collective-permute-start(bf16[3,104,800]{2,1,0:T(8,128)(2,1)S(1)} %fusion.6), channel_id=1, source_target_pairs={{0,2},{1,3},{2,0},{3,1},{4,6},{5,7},{6,4},{7,5},{8,10},{9,11},{10,... | collective-permute-start | bytes 1497608 | tf_op jit(solution)/shard_map/ppermute | solution.py:27
  374.6 14.8 %collective-permute-start.43 = (f32[104,1600]{1,0:T(8,128)S(1)}, f32[104,1600]{1,0:T(8,128)S(1)}, u32[]{:S(2)}, u32[]{:S(2)}) collective-permute-start(f32[104,1600]{1,0:T(8,128)S(1)} %convert_add_fusion.2), channel_id=1, source_target_pairs={{0,1},{1,0},{2,3},{3,2},{4,5},{5,4},{6,7},{7,6},{8,9},{9,8},{10,11... | collective-permute-start | bytes 1996808 | tf_op jit(solution)/shard_map/ppermute | solution.py:27
  383.8 29.7 %collective-permute-start.26 = (f32[208,800]{1,0:T(8,128)S(1)}, f32[208,800]{1,0:T(8,128)S(1)}, u32[]{:S(2)}, u32[]{:S(2)}) collective-permute-start(f32[208,800]{1,0:T(8,128)S(1)} %convert_add_fusion.1), channel_id=1, source_target_pairs={{0,1},{1,0},{2,3},{3,2},{4,5},{5,4},{6,7},{7,6},{8,9},{9,8},{10,11... | collective-permute-start | bytes 1996808 | tf_op jit(solution)/shard_map/ppermute | solution.py:27
  385.2 26.8 %collective-permute-start.36 = (bf16[3,104,800]{2,1,0:T(8,128)(2,1)S(1)}, bf16[3,104,800]{2,1,0:T(8,128)(2,1)S(1)}, u32[]{:S(2)}, u32[]{:S(2)}) collective-permute-start(bf16[3,104,800]{2,1,0:T(8,128)(2,1)S(1)} %add_convert_fusion), channel_id=1, source_target_pairs={{0,4},{1,5},{2,6},{3,7},{4,0},{5,1},{6,2},{7,3},{8,12},{9,13},{10,... | collective-permute-start | bytes 1497608 | tf_op jit(solution)/shard_map/ppermute | solution.py:27
  (57 other events, 755.5 us)
